TPU v7x, 32 devices: a whole 2x2x4 slice. The times are simulated.
32 devices in a mesh: dp: 8 (over z, x), tensor: 4 (over y, core).
Axes of the slice: x: 2, y: 2, z: 4, core: 2. Of those that a mesh axis runs over, the one named last changes fastest.
Arguments:
- inputs: bfloat16 [8192, 1024], P(('dp', 'tensor')), may hold values from -6 to 6, as said below
- teacher: bfloat16 [8192, 1024], P(('dp', 'tensor')), may hold values from -9 to 9, as said below
- query_weight: bfloat16 [1024, 1024], P('dp', 'tensor'), may hold values from -0.25 to 0.25
- key_weight: bfloat16 [1024, 1024], P('dp', 'tensor'), may hold values from -0.25 to 0.25
- value_weight: bfloat16 [1024, 1024], P('dp', 'tensor'), may hold values from -0.1875 to 0.1875
- out_weight: bfloat16 [1024, 1024], P('tensor', 'dp'), may hold values from -1 to 1
- up_weight: bfloat16 [1024, 4096], P('dp', 'tensor'), may hold values from -0.1875 to 0.1875
- down_weight: bfloat16 [4096, 1024], P('tensor', 'dp'), may hold values from -0.125 to 0.125
- query_bias: float32 [1024], replicated, may hold values from -3 to 3
- value_bias: float32 [1024], replicated, may hold values from -0.18 to 0.18
- out_bias: float32 [1024], replicated, may hold values from -0.3 to 0.3
- up_bias: float32 [4096], replicated, may hold values from -1.2 to -0.6
- down_bias: float32 [1024], replicated, may hold values from -0.3 to 0.3
- first_gain: float32 [1024], replicated, may hold values from 0.5 to 1.5
- first_shift: float32 [1024], replicated, may hold values from -0.3 to 0.3
- second_gain: float32 [1024], replicated, may hold values from 0.5 to 1.5
- second_shift: float32 [1024], replicated, may hold values from -0.3 to 0.3
Outputs:
- output: bfloat16 [8192, 1024], P(('dp', 'tensor'))
- loss: float32 [], replicated
- grad_inputs: float32 [8192, 1024], P(('dp', 'tensor'))
- grad_query_weight: float32 [1024, 1024], P('dp', 'tensor')
- grad_key_weight: float32 [1024, 1024], P('dp', 'tensor')
- grad_value_weight: float32 [1024, 1024], P('dp', 'tensor')
- grad_out_weight: float32 [1024, 1024], P('tensor', 'dp')
- grad_up_weight: float32 [1024, 4096], P('dp', 'tensor')
- grad_down_weight: float32 [4096, 1024], P('tensor', 'dp')
- grad_query_bias: float32 [1024], replicated
- grad_value_bias: float32 [1024], replicated
- grad_out_bias: float32 [1024], replicated
- grad_up_bias: float32 [4096], replicated
- grad_down_bias: float32 [1024], replicated
- grad_first_gain: float32 [1024], replicated
- grad_first_shift: float32 [1024], replicated
- grad_second_gain: float32 [1024], replicated
- grad_second_shift: float32 [1024], replicated
Inputs may be any that keep to these rules, and one draw needn't show every extreme that they name: `inputs`: states of order one. `teacher`: target states of order one.
All inputs are finite; a program needn't handle non-finite values.
Results may differ from a plain program's by a relative error of at most 0.02.
Values may be sent and summed in bfloat16 or wider, within the bound.
A program may use at most 128 MiB of HBM per device.

v0:
```python
import math

import jax
import jax.numpy as jnp
from jax import lax
from jax.sharding import PartitionSpec as P

HEAD_DIM = 64
SEQ = 512


EPSILON = 1e-05


def layer_norm(values, gain, shift):
    center = values - jnp.mean(values, axis=-1, keepdims=True)
    scaling = lax.rsqrt(jnp.mean(center * center, axis=-1, keepdims=True) + EPSILON)
    normed = center * scaling
    return (normed * gain + shift, normed, scaling)


def norm_backward(upstream, normed, scaling, gain):
    scaled = upstream * gain
    across = scaling * (
        scaled
        - jnp.mean(scaled, axis=-1, keepdims=True)
        - normed * jnp.mean(scaled * normed, axis=-1, keepdims=True)
    )
    return (across, jnp.sum(upstream * normed, axis=0), jnp.sum(upstream, axis=0))


def placed(vector, full_length, offset):
    return lax.dynamic_update_slice(jnp.zeros((full_length,), jnp.float32), vector, (offset,))


def shards(
    inputs,
    teacher,
    query_weight,
    key_weight,
    value_weight,
    out_weight,
    up_weight,
    down_weight,
    query_bias,
    value_bias,
    out_bias,
    up_bias,
    down_bias,
    first_gain,
    first_shift,
    second_gain,
    second_shift,
):
    full_query, full_key, full_value, full_up, full_out, full_down = (
        lax.all_gather(query_weight, "dp", axis=0, tiled=True),
        lax.all_gather(key_weight, "dp", axis=0, tiled=True),
        lax.all_gather(value_weight, "dp", axis=0, tiled=True),
        lax.all_gather(up_weight, "dp", axis=0, tiled=True),
        lax.all_gather(out_weight, "dp", axis=1, tiled=True),
        lax.all_gather(down_weight, "dp", axis=1, tiled=True),
    )
    slot = lax.axis_index("tensor")
    head_width = full_query.shape[1]
    inner_width = full_up.shape[1]
    model_width = inputs.shape[1]
    local_rows = inputs.shape[0]
    bias_query = lax.dynamic_slice_in_dim(query_bias, slot * head_width, head_width)
    bias_value = lax.dynamic_slice_in_dim(value_bias, slot * head_width, head_width)
    bias_up = lax.dynamic_slice_in_dim(up_bias, slot * inner_width, inner_width)
    scaling_factor = 1.0 / math.sqrt(HEAD_DIM)
    seen = lax.all_gather(inputs, "tensor", axis=0, tiled=True)
    seq_count = seen.shape[0] // SEQ
    head_count = head_width // HEAD_DIM
    query = (jnp.dot(seen, full_query, preferred_element_type=jnp.float32) + bias_query).astype(
        jnp.bfloat16
    )
    keys = jnp.dot(seen, full_key, preferred_element_type=jnp.float32).astype(jnp.bfloat16)
    values = (jnp.dot(seen, full_value, preferred_element_type=jnp.float32) + bias_value).astype(
        jnp.bfloat16
    )
    query_heads = query.reshape(seq_count, SEQ, head_count, HEAD_DIM)
    key_heads = keys.reshape(seq_count, SEQ, head_count, HEAD_DIM)
    value_heads = values.reshape(seq_count, SEQ, head_count, HEAD_DIM)
    scores = (
        jnp.einsum("bqhd,bkhd->bhqk", query_heads, key_heads, preferred_element_type=jnp.float32)
        * scaling_factor
    )
    highest = jnp.max(scores, axis=-1, keepdims=True)
    weights = jnp.exp(scores - highest)
    totals = jnp.sum(weights, axis=-1, keepdims=True)
    log_total = highest + jnp.log(totals)
    probs_low = (weights / totals).astype(jnp.bfloat16)
    context = (
        jnp.einsum("bhqk,bkhd->bqhd", probs_low, value_heads, preferred_element_type=jnp.float32)
        .reshape(-1, head_width)
        .astype(jnp.bfloat16)
    )
    block = context
    attended = (
        lax.psum_scatter(
            jnp.dot(block, full_out, preferred_element_type=jnp.float32).astype(jnp.bfloat16),
            "tensor",
            scatter_dimension=0,
            tiled=True,
        ).astype(jnp.float32)
        + out_bias
    )
    first = inputs.astype(jnp.float32) + attended
    hidden, normed_one, scaling_one = layer_norm(first, first_gain, first_shift)
    spread = lax.all_gather(hidden.astype(jnp.bfloat16), "tensor", axis=0, tiled=True)
    upper = jnp.dot(spread, full_up, preferred_element_type=jnp.float32) + bias_up
    erf_part = jax.scipy.special.erf(upper / math.sqrt(2.0))
    activated = (0.5 * upper * (1.0 + erf_part)).astype(jnp.bfloat16)
    block = activated
    second = (
        hidden
        + lax.psum_scatter(
            jnp.dot(block, full_down, preferred_element_type=jnp.float32).astype(jnp.bfloat16),
            "tensor",
            scatter_dimension=0,
            tiled=True,
        ).astype(jnp.float32)
        + down_bias
    )
    result, normed_two, scaling_two = layer_norm(second, second_gain, second_shift)
    diff = result - teacher.astype(jnp.float32)
    loss_part = 0.5 * jnp.sum(diff * diff)
    grad_second, grad_gain_two, grad_shift_two = norm_backward(
        diff, normed_two, scaling_two, second_gain
    )
    mixed_all = lax.all_gather(grad_second.astype(jnp.bfloat16), "tensor", axis=0, tiled=True)
    grad_act = jnp.einsum("td,fd->tf", mixed_all, full_down, preferred_element_type=jnp.float32)
    slope = 0.5 * (1.0 + erf_part) + upper * jnp.exp(-0.5 * upper * upper) / math.sqrt(
        2.0 * math.pi
    )
    grad_upper = (grad_act * slope).astype(jnp.bfloat16)
    grad_down = jnp.einsum("tf,td->fd", activated, mixed_all, preferred_element_type=jnp.float32)
    grad_up = jnp.einsum("td,tf->df", spread, grad_upper, preferred_element_type=jnp.float32)
    sum_up_bias = jnp.sum(grad_upper.astype(jnp.float32), axis=0)
    block = grad_upper
    grad_hidden = grad_second + lax.psum_scatter(
        jnp.einsum("tf,df->td", block, full_up, preferred_element_type=jnp.float32).astype(
            jnp.bfloat16
        ),
        "tensor",
        scatter_dimension=0,
        tiled=True,
    ).astype(jnp.float32)
    grad_first, grad_gain_one, grad_shift_one = norm_backward(
        grad_hidden, normed_one, scaling_one, first_gain
    )
    attended_all = lax.all_gather(grad_first.astype(jnp.bfloat16), "tensor", axis=0, tiled=True)
    grad_context = jnp.einsum(
        "td,wd->tw", attended_all, full_out, preferred_element_type=jnp.float32
    ).astype(jnp.bfloat16)
    grad_out = jnp.einsum("tw,td->wd", context, attended_all, preferred_element_type=jnp.float32)
    again = (
        jnp.einsum("bqhd,bkhd->bhqk", query_heads, key_heads, preferred_element_type=jnp.float32)
        * scaling_factor
    )
    probs_again = jnp.exp(again - log_total)
    context_heads = grad_context.reshape(seq_count, SEQ, head_count, HEAD_DIM)
    grad_probs = jnp.einsum(
        "bqhd,bkhd->bhqk", context_heads, value_heads, preferred_element_type=jnp.float32
    )
    inner_sum = jnp.sum(probs_again * grad_probs, axis=-1, keepdims=True)
    grad_scores = (probs_again * (grad_probs - inner_sum)).astype(jnp.bfloat16)
    grad_values = (
        jnp.einsum(
            "bhqk,bqhd->bkhd",
            probs_again.astype(jnp.bfloat16),
            context_heads,
            preferred_element_type=jnp.float32,
        )
        .reshape(-1, head_width)
        .astype(jnp.bfloat16)
    )
    grad_query = (
        (
            jnp.einsum(
                "bhqk,bkhd->bqhd", grad_scores, key_heads, preferred_element_type=jnp.float32
            )
            * scaling_factor
        )
        .reshape(-1, head_width)
        .astype(jnp.bfloat16)
    )
    grad_keys = (
        (
            jnp.einsum(
                "bhqk,bqhd->bkhd", grad_scores, query_heads, preferred_element_type=jnp.float32
            )
            * scaling_factor
        )
        .reshape(-1, head_width)
        .astype(jnp.bfloat16)
    )
    grad_qw = jnp.einsum("td,tw->dw", seen, grad_query, preferred_element_type=jnp.float32)
    grad_kw = jnp.einsum("td,tw->dw", seen, grad_keys, preferred_element_type=jnp.float32)
    grad_vw = jnp.einsum("td,tw->dw", seen, grad_values, preferred_element_type=jnp.float32)
    sum_query_bias = jnp.sum(grad_query.astype(jnp.float32), axis=0)
    sum_value_bias = jnp.sum(grad_values.astype(jnp.float32), axis=0)
    total_term = jnp.einsum("tw,dw->td", grad_query, full_query, preferred_element_type=jnp.float32)
    total_term = total_term + jnp.einsum(
        "tw,dw->td", grad_keys, full_key, preferred_element_type=jnp.float32
    )
    grad_inputs = grad_first + lax.psum_scatter(
        (
            total_term
            + jnp.einsum("tw,dw->td", grad_values, full_value, preferred_element_type=jnp.float32)
        ).astype(jnp.bfloat16),
        "tensor",
        scatter_dimension=0,
        tiled=True,
    ).astype(jnp.float32)
    shard_query, shard_key, shard_value, shard_up, shard_out, shard_down = (
        lax.psum_scatter(grad_qw, "dp", scatter_dimension=0, tiled=True),
        lax.psum_scatter(grad_kw, "dp", scatter_dimension=0, tiled=True),
        lax.psum_scatter(grad_vw, "dp", scatter_dimension=0, tiled=True),
        lax.psum_scatter(grad_up, "dp", scatter_dimension=0, tiled=True),
        lax.psum_scatter(grad_out, "dp", scatter_dimension=1, tiled=True),
        lax.psum_scatter(grad_down, "dp", scatter_dimension=1, tiled=True),
    )
    summed = lax.psum(
        (
            loss_part,
            placed(sum_query_bias, model_width, slot * head_width),
            placed(sum_value_bias, model_width, slot * head_width),
            jnp.sum(grad_first, axis=0),
            placed(sum_up_bias, up_bias.shape[0], slot * inner_width),
            jnp.sum(grad_second, axis=0),
            grad_gain_one,
            grad_shift_one,
            grad_gain_two,
            grad_shift_two,
        ),
        ("dp", "tensor"),
    )
    token_total = local_rows * lax.axis_size("dp") * lax.axis_size("tensor")
    loss = summed[0] / token_total
    return (
        result.astype(jnp.bfloat16),
        loss,
        grad_inputs,
        shard_query,
        shard_key,
        shard_value,
        shard_out,
        shard_up,
        shard_down,
        summed[1],
        summed[2],
        summed[3],
        summed[4],
        summed[5],
        summed[6],
        summed[7],
        summed[8],
        summed[9],
    )


def solution(mesh):
    in_specs = (
        P(("dp", "tensor"), None),
        P(("dp", "tensor"), None),
        P("dp", "tensor"),
        P("dp", "tensor"),
        P("dp", "tensor"),
        P("tensor", "dp"),
        P("dp", "tensor"),
        P("tensor", "dp"),
        P(),
        P(),
        P(),
        P(),
        P(),
        P(),
        P(),
        P(),
        P(),
    )
    out_specs = (
        P(("dp", "tensor"), None),
        P(),
        P(("dp", "tensor"), None),
        P("dp", "tensor"),
        P("dp", "tensor"),
        P("dp", "tensor"),
        P("tensor", "dp"),
        P("dp", "tensor"),
        P("tensor", "dp"),
        P(),
        P(),
        P(),
        P(),
        P(),
        P(),
        P(),
        P(),
        P(),
    )
    return jax.shard_map(shards, mesh=mesh, in_specs=in_specs, out_specs=out_specs, check_vma=False)
```

profile of v0, /device:TPU:0, one launch (start us, length us, event | category | flops | bytes accessed | tf_op | source)
XLA Modules:
  0.0 935.9 jit_solution(4503676397369829815)
XLA Ops:
  10.3 35.4 %all_gather.32 = bf16[1024,256]{1,0:T(8,128)(2,1)} all-gather(bf16[128,256]{1,0:T(8,128)(2,1)} %param.19), channel_id=1, replica_groups=mesh['dp'=8,'tensor'=4] {'dp'}, dimensions={0}, use_global_device_ids=true | all-gather | bytes 589824 | tf_op jit(solution)/shard_map/all_gather | solution.py:56
  45.8 33.6 %all_gather.33 = bf16[1024,256]{1,0:T(8,128)(2,1)} all-gather(bf16[128,256]{1,0:T(8,128)(2,1)} %param.20), channel_id=1, replica_groups=mesh['dp'=8,'tensor'=4] {'dp'}, dimensions={0}, use_global_device_ids=true | all-gather | bytes 589824 | tf_op jit(solution)/shard_map/all_gather | solution.py:57
  79.4 31.9 %all_gather.31 = bf16[1024,256]{1,0:T(8,128)(2,1)S(1)} all-gather(bf16[128,256]{1,0:T(8,128)(2,1)} %param.21), channel_id=1, replica_groups=mesh['dp'=8,'tensor'=4] {'dp'}, dimensions={0}, use_global_device_ids=true | all-gather | bytes 589824 | tf_op jit(solution)/shard_map/all_gather | solution.py:58
  111.2 28.3 %all_gather.34 = bf16[256,1024]{1,0:T(8,128)(2,1)} all-gather(bf16[256,128]{1,0:T(8,128)(2,1)} %param.22), channel_id=1, replica_groups=mesh['dp'=8,'tensor'=4] {'dp'}, dimensions={1}, use_global_device_ids=true | all-gather | bytes 589824 | tf_op jit(solution)/shard_map/all_gather | solution.py:60
  139.6 3.2 fusion.14
  142.8 2.0 reshape.122
  146.2 1.8 convolution_convert_fusion.4
  152.5 2.8 reshape.123
  159.6 1.8 copy-done
  161.4 2.0 fusion.22
  164.8 2.1 convolution_convert_fusion.2
  167.6 30.0 %reduce-scatter.11.cloned.1.call-done = bf16[256,1024]{1,0:T(8,128)(2,1)} async-done(((bf16[1024,1024]{1,0:T(8,128)(2,1)}), bf16[256,1024]{1,0:T(8,128)(2,1)}) %reduce-scatter.11.cloned.1.call-update) | async-done | bytes 524304 | tf_op jit(solution)/shard_map/reduce_scatter | solution.py:101
  200.3 2.1 fusion.23
  204.0 13.9 %all-gather.11.cloned.1.call-done = bf16[1024,1024]{1,0:T(8,128)(2,1)} async-done(((bf16[128,1024]{1,0:T(8,128)(2,1)}), bf16[1024,1024]{1,0:T(8,128)(2,1)}) %all-gather.11.cloned.1.call-update) | async-done | bytes 2097168 | tf_op jit(solution)/shard_map/all_gather | solution.py:59
  217.9 23.1 %all-gather.9.cloned.1.call-done = bf16[1024,1024]{1,0:T(8,128)(2,1)} async-done(((bf16[256,1024]{1,0:T(8,128)(2,1)}), bf16[1024,1024]{1,0:T(8,128)(2,1)}) %all-gather.9.cloned.1.call-update) | async-done | bytes 2097168 | tf_op jit(solution)/shard_map/all_gather | solution.py:111
  240.9 7.4 multiply_convert_fusion.1
  248.3 45.0 %all-gather.13.cloned.1.call-done = bf16[1024,1024]{1,0:T(8,128)(2,1)} async-done(((bf16[1024,128]{1,0:T(8,128)(2,1)}), bf16[1024,1024]{1,0:T(8,128)(2,1)}) %all-gather.13.cloned.1.call-update) | async-done | bytes 2097168 | tf_op jit(solution)/shard_map/all_gather | solution.py:61
  293.3 6.0 convolution_convert_fusion.1
  299.4 29.4 %reduce-scatter.13.cloned.1.call-done = bf16[256,1024]{1,0:T(8,128)(2,1)} async-done(((bf16[1024,1024]{1,0:T(8,128)(2,1)}), bf16[256,1024]{1,0:T(8,128)(2,1)}) %reduce-scatter.13.cloned.1.call-update) | async-done | bytes 524304 | tf_op jit(solution)/shard_map/reduce_scatter | solution.py:118
  330.8 2.5 fusion.29
  333.2 1.8 fusion.31
  335.1 22.5 %all-gather.15.cloned.1.call-done = bf16[1024,1024]{1,0:T(8,128)(2,1)} async-done(((bf16[256,1024]{1,0:T(8,128)(2,1)}), bf16[1024,1024]{1,0:T(8,128)(2,1)}) %all-gather.15.cloned.1.call-update) | async-done | bytes 2097168 | tf_op jit(solution)/shard_map/all_gather | solution.py:132
  357.6 6.6 convert_reduce_fusion
  365.7 3.7 convolution_convert_fusion
  369.4 31.3 %reduce-scatter.15.cloned.1.call-done = bf16[256,1024]{1,0:T(8,128)(2,1)} async-done(((bf16[1024,1024]{1,0:T(8,128)(2,1)}), bf16[256,1024]{1,0:T(8,128)(2,1)}) %reduce-scatter.15.cloned.1.call-update) | async-done | bytes 524304 | tf_op jit(solution)/shard_map/reduce_scatter | solution.py:142
  400.7 2.1 multiply_reduce_fusion.3
  402.8 1.9 fusion.30
  406.9 22.3 %all-gather.17.cloned.1.call-done = bf16[1024,1024]{1,0:T(8,128)(2,1)} async-done(((bf16[256,1024]{1,0:T(8,128)(2,1)}), bf16[1024,1024]{1,0:T(8,128)(2,1)}) %all-gather.17.cloned.1.call-update) | async-done | bytes 2097168 | tf_op jit(solution)/shard_map/all_gather | solution.py:153
  429.1 2.4 convolution_convert_fusion.3
  434.5 5.0 convert_reduce_fusion.1
  440.2 1.7 convolution_bitcast_fusion
  442.0 4.8 multiply_reduce_fusion
  446.8 4.8 multiply_convert_fusion
  451.6 1.9 copy-done.1
  457.6 3.6 fusion.21
  464.7 1.9 fusion.33
  467.4 2.1 add_convert_fusion
  469.5 6.5 fusion.37
  477.7 6.0 fusion.36
  484.7 3.4 fusion.35
  489.6 40.9 %all-reduce = (f32[]{:T(128)}, f32[1024]{0:T(1024)}, f32[1024]{0:T(1024)}, f32[1024]{0:T(1024)}, f32[4096]{0:T(1024)}, /*index=5*/f32[1024]{0:T(1024)}, f32[1024...) all-reduce(f32[]{:T(128)S(6)} %mul.164, ...), channel_id=1, replica_groups=mesh['dp'=8,'tensor'=4] {'dp','tensor'}, use_global_device_ids=true, to_apply=%region_9.0 | all-reduce | flops 12289 | bytes 98312 | tf_op jit(solution)/shard_map/psum | solution.py:225
  532.9 41.5 %reduce-scatter.19.cloned.1.call-done = f32[128,256]{0,1:T(8,128)} async-done(((f32[1024,256]{0,1:T(8,128)}), f32[128,256]{0,1:T(8,128)}) %reduce-scatter.19.cloned.1.call-update) | async-done | bytes 131088 | tf_op jit(solution)/shard_map/reduce_scatter | solution.py:218
  576.0 65.4 %reduce-scatter.21.cloned.1.call-done = f32[128,256]{0,1:T(8,128)} async-done(((f32[1024,256]{0,1:T(8,128)}), f32[128,256]{0,1:T(8,128)}) %reduce-scatter.21.cloned.1.call-update) | async-done | bytes 131088 | tf_op jit(solution)/shard_map/reduce_scatter | solution.py:219
  643.1 30.9 %reduce-scatter.17.cloned.1.call-done = bf16[256,1024]{1,0:T(8,128)(2,1)} async-done(((bf16[1024,1024]{1,0:T(8,128)(2,1)}), bf16[256,1024]{1,0:T(8,128)(2,1)}) %reduce-scatter.17.cloned.1.call-update) | async-done | bytes 524304 | tf_op jit(solution)/shard_map/reduce_scatter | solution.py:208
  674.0 2.2 convert_add_fusion
  676.2 90.7 %reduce-scatter.29.cloned.1.call-done = f32[1024,128]{1,0:T(8,128)} async-done(((f32[1024,1024]{1,0:T(8,128)}), f32[1024,128]{1,0:T(8,128)}) %reduce-scatter.29.cloned.1.call-update) | async-done | bytes 524304 | tf_op jit(solution)/shard_map/reduce_scatter | solution.py:223
  766.9 91.9 %reduce-scatter.27.cloned.1.call-done = f32[128,1024]{1,0:T(8,128)} async-done(((f32[1024,1024]{1,0:T(8,128)}), f32[128,1024]{1,0:T(8,128)}) %reduce-scatter.27.cloned.1.call-update) | async-done | bytes 524304 | tf_op jit(solution)/shard_map/reduce_scatter | solution.py:221
  858.8 68.3 %reduce-scatter.25.cloned.1.call-done = f32[256,128]{1,0:T(8,128)} async-done(((f32[256,1024]{1,0:T(8,128)}), f32[256,128]{1,0:T(8,128)}) %reduce-scatter.25.cloned.1.call-update) | async-done | bytes 131088 | tf_op jit(solution)/shard_map/reduce_scatter | solution.py:222
  (146 shorter events, 44.6 us)
Async XLA Ops:
  8.0 131.5 %all-gather.7.cloned.1.call-start = ((), (), s32[]{:S(2)}) async-start(), calls=%async_computation.10 | async-start | bytes 2621440 | tf_op jit(solution)/shard_map/all_gather | solution.py:72
  8.8 188.9 %reduce-scatter.11.cloned.1.call-start = ((), (), s32[]{:S(2)}) async-start(), calls=%async_computation.11 | async-start | bytes 2621440 | tf_op jit(solution)/shard_map/reduce_scatter | solution.py:101
  111.2 28.3 %copy-start.18 = (bf16[1024,256]{1,0:T(8,128)(2,1)}, bf16[1024,256]{1,0:T(8,128)(2,1)S(1)}, u32[]{:S(2)}) copy-start(bf16[1024,256]{1,0:T(8,128)(2,1)S(1)} %all_gather.31) | copy-start | bytes 1572868
  139.5 6.6 copy-start.3
  146.2 4.8 copy-start.21
  151.0 5.9 copy-start.9
  156.8 1.3 copy-start.7
  158.2 3.2 copy-start
  158.2 3.2 copy-start.17
  161.4 3.5 copy-start.23
  163.4 34.3 %copy-start.2 = (bf16[256,1024]{1,0:T(8,128)(2,1)S(1)}, bf16[256,1024]{1,0:T(8,128)(2,1)}, u32[]{:S(2)}) copy-start(bf16[256,1024]{1,0:T(8,128)(2,1)} %param.17) | copy-start | bytes 1572868
  163.4 34.3 %copy-start.24 = (f32[1024]{0:T(1024)S(1)}, f32[1024]{0:T(1024)}, u32[]{:S(2)}) copy-start(f32[1024]{0:T(1024)} %param.27) | copy-start | bytes 12292
  163.9 36.4 %copy-start.25 = (f32[1024]{0:T(1024)S(1)}, f32[1024]{0:T(1024)}, u32[]{:S(2)}) copy-start(f32[1024]{0:T(1024)} %param.30) | copy-start | bytes 12292
  164.0 36.4 %copy-start.26 = (f32[1024]{0:T(1024)S(1)}, f32[1024]{0:T(1024)}, u32[]{:S(2)}) copy-start(f32[1024]{0:T(1024)} %param.31) | copy-start | bytes 12292
  167.0 50.9 %all-gather.11.cloned.1.call-start = ((), (), s32[]{:S(2)}) async-start(), calls=%async_computation.13 | async-start | bytes 2359296 | tf_op jit(solution)/shard_map/all_gather | solution.py:59
  167.6 73.4 %all-gather.9.cloned.1.call-start = ((), (), s32[]{:S(2)}) async-start(), calls=%async_computation.12 | async-start | bytes 2621440 | tf_op jit(solution)/shard_map/all_gather | solution.py:111
  202.5 90.8 %all-gather.13.cloned.1.call-start = ((), (), s32[]{:S(2)}) async-start(), calls=%async_computation.14 | async-start | bytes 2359296 | tf_op jit(solution)/shard_map/all_gather | solution.py:61
  203.1 125.7 %reduce-scatter.13.cloned.1.call-start = ((), (), s32[]{:S(2)}) async-start(), calls=%async_computation.15 | async-start | bytes 2621440 | tf_op jit(solution)/shard_map/reduce_scatter | solution.py:118
  293.3 35.5 %copy-start.4 = (bf16[256,1024]{1,0:T(8,128)(2,1)S(1)}, bf16[256,1024]{1,0:T(8,128)(2,1)}, u32[]{:S(2)}) copy-start(bf16[256,1024]{1,0:T(8,128)(2,1)} %reduce-scatter.11.cloned.1.call-done) | copy-start | bytes 1572868
  293.3 35.5 %copy-start.29 = (f32[1024]{0:T(1024)S(1)}, f32[1024]{0:T(1024)}, u32[]{:S(2)}) copy-start(f32[1024]{0:T(1024)} %param.29) | copy-start | bytes 12292
  299.3 31.4 %copy-start.27 = (f32[1024]{0:T(1024)S(1)}, f32[1024]{0:T(1024)}, u32[]{:S(2)}) copy-start(f32[1024]{0:T(1024)} %param.33) | copy-start | bytes 12292
  299.3 31.5 %copy-start.28 = (f32[1024]{0:T(1024)S(1)}, f32[1024]{0:T(1024)}, u32[]{:S(2)}) copy-start(f32[1024]{0:T(1024)} %param.32) | copy-start | bytes 12292
  299.3 58.3 %all-gather.15.cloned.1.call-start = ((), (), s32[]{:S(2)}) async-start(), calls=%async_computation.16 | async-start | bytes 2621440 | tf_op jit(solution)/shard_map/all_gather | solution.py:132
  328.8 4.4 copy-start.22
  335.1 65.6 %reduce-scatter.15.cloned.1.call-start = ((), (), s32[]{:S(2)}) async-start(), calls=%async_computation.17 | async-start | bytes 2621440 | tf_op jit(solution)/shard_map/reduce_scatter | solution.py:142
  357.6 8.1 copy-start.31
  364.3 1.4 copy-start.32
  369.4 59.7 %all-gather.17.cloned.1.call-start = ((), (), s32[]{:S(2)}) async-start(), calls=%async_computation.18 | async-start | bytes 2621440 | tf_op jit(solution)/shard_map/all_gather | solution.py:153
  404.7 1.0 copy-start.5
  406.6 124.6 %reduce-scatter.23.cloned.1.call-start = ((), (), s32[]{:S(2)}) async-start(), calls=%async_computation.22 | async-start | bytes 1179648 | tf_op jit(solution)/shard_map/reduce_scatter | solution.py:220
  441.9 132.5 %reduce-scatter.19.cloned.1.call-start = ((), (), s32[]{:S(2)}) async-start(), calls=%async_computation.20 | async-start | bytes 1179648 | tf_op jit(solution)/shard_map/reduce_scatter | solution.py:218
  446.8 6.7 copy-start.10
  451.6 1.9 copy-start.1
  454.4 3.2 copy-start.8
  455.0 0.8 copy-start.11
  457.5 183.9 %reduce-scatter.21.cloned.1.call-start = ((), (), s32[]{:S(2)}) async-start(), calls=%async_computation.21 | async-start | bytes 1179648 | tf_op jit(solution)/shard_map/reduce_scatter | solution.py:219
  461.2 3.5 copy-start.12
  461.8 0.8 copy-start.13
  464.3 2.3 copy-start.14
  464.3 2.3 copy-start.20
  464.3 3.0 copy-start.19
  464.4 209.7 %reduce-scatter.17.cloned.1.call-start = ((), (), s32[]{:S(2)}) async-start(), calls=%async_computation.19 | async-start | bytes 2621440 | tf_op jit(solution)/shard_map/reduce_scatter | solution.py:208
  469.5 297.4 %reduce-scatter.29.cloned.1.call-start = ((), (), s32[]{:S(2)}) async-start(), calls=%async_computation.25 | async-start | bytes 4718592 | tf_op jit(solution)/shard_map/reduce_scatter | solution.py:223
  476.1 1.6 copy-start.30
  476.1 382.7 %reduce-scatter.27.cloned.1.call-start = ((), (), s32[]{:S(2)}) async-start(), calls=%async_computation.24 | async-start | bytes 4718592 | tf_op jit(solution)/shard_map/reduce_scatter | solution.py:221
  483.6 1.0 copy-start.16
  483.6 190.4 %copy-start.6 = (f32[256,1024]{1,0:T(8,128)S(1)}, f32[256,1024]{1,0:T(8,128)}, u32[]{:S(2)}) copy-start(f32[256,1024]{1,0:T(8,128)} %copy-done.5) | copy-start | bytes 3145732
  483.7 443.5 %reduce-scatter.25.cloned.1.call-start = ((), (), s32[]{:S(2)}) async-start(), calls=%async_computation.23 | async-start | bytes 1179648 | tf_op jit(solution)/shard_map/reduce_scatter | solution.py:222
  (1 other events, 0.8 us)
Sparse Core Ops, SparseCore 0:
  10.4 25.2 all-gather.6
  167.1 30.4 reduce-scatter.10
  299.5 29.3 reduce-scatter.12
  369.5 31.1 reduce-scatter.14
Sparse Core Ops, SparseCore 1:
  169.6 48.2 all-gather.10
  219.9 21.0 all-gather.8
  242.9 50.4 all-gather.12
  335.2 22.4 all-gather.14
  406.7 22.4 all-gather.16
  442.0 64.8 reduce-scatter.22
  510.7 63.6 reduce-scatter.18
  577.7 63.7 reduce-scatter.20
  643.8 30.1 reduce-scatter.16
  678.2 88.6 reduce-scatter.28
  771.0 87.8 reduce-scatter.26
  862.8 64.3 reduce-scatter.24
where the time goes:
time: 945 us; the launch traced here: 936 us
  waiting for transfers between devices  608 us (64%)
  blocking collectives  170 us (18%)
  matrix products  78.1 us (8%)
  local copies, waits for them, and re-layouts  35.1 us (4%)
  other arithmetic  24.3 us (3%)
  between operations  18.8 us (2%)
    reduce_scatter x1, waiting for transfers between devices, shards(): lax.psum_scatter(grad_up, 'dp', scatter_dimension=0, tiled=True)  91.9 us
    reduce_scatter x1, waiting for transfers between devices, shards(): lax.psum_scatter(grad_down, 'dp', scatter_dimension=1, tiled=True)  90.7 us
    reduce_scatter x1, waiting for transfers between devices, shards(): lax.psum_scatter(grad_out, 'dp', scatter_dimension=1, tiled=True)  68.3 us
    reduce_scatter x1, waiting for transfers between devices, shards(): lax.psum_scatter(grad_kw, 'dp', scatter_dimension=0, tiled=True)  65.4 us
    all_gather x1, waiting for transfers between devices, shards(): lax.all_gather(down_weight, 'dp', axis=1, tiled=True)  45 us
    reduce_scatter x1, waiting for transfers between devices, shards(): lax.psum_scatter(grad_qw, 'dp', scatter_dimension=0, tiled=True)  41.5 us
    psum x1, blocking collectives, shards(): lax.psum((loss_part, placed(sum_query_bias, model_width, slot * head_widt...  40.9 us
    all_gather x1, blocking collectives, shards(): lax.all_gather(query_weight, 'dp', axis=0, tiled=True)  35.4 us
  transfers between devices with their start and end apart: 16, of which 14 were waited for; matrix products, arithmetic and copies ran while one was open for 7% of the time, Pallas kernels for 0%

commit v1 on v0

v1 whole, which is shorter than its diff:
```python
import functools
import math

import jax
import jax.numpy as jnp
from jax import lax
from jax.experimental import pallas as pl
from jax.experimental.pallas import tpu as pltpu
from jax.sharding import PartitionSpec as P

HEAD_DIM = 64
SEQ = 512
EPSILON = 1e-05
MESH = pl.DeviceIdType.MESH
F32 = jnp.float32
BF16 = jnp.bfloat16
NN = ((1,), (0,))
NT = ((1,), (1,))
TN = ((0,), (0,))
CHUNK = 32
ROOT_TWO = math.sqrt(2.0)
ROOT_TWO_PI = math.sqrt(2.0 * math.pi)
VECTORS = 16


def dot(left, right, dims):
    return lax.dot_general(left, right, (dims, ((), ())), preferred_element_type=F32)


def remote(src, dst, send, recv, peer):
    return pltpu.make_async_remote_copy(
        src_ref=src, dst_ref=dst, send_sem=send, recv_sem=recv, device_id=peer, device_id_type=MESH
    )


class Place:
    def __init__(self, outer):
        self.outer = outer
        self.dp = lax.axis_index("dp")
        self.t = lax.axis_index("tensor")
        self.z, self.x = self.dp // 2, self.dp % 2
        self.y, self.c = self.t // 2, self.t % 2
        self.x_peer = (self.z * 2 + 1 - self.x, self.t)
        self.y_peer = (self.dp, (1 - self.y) * 2 + self.c)
        self.c_peer = (self.dp, self.y * 2 + 1 - self.c)
        self.diag = (1 - self.y) * 2 + 1 - self.c
        self.diag_peer = (self.dp, self.diag)

    def z_peer(self, step):
        return (lax.rem(self.z + step, self.outer) * 2 + self.x, self.t)

    def enter(self):
        barrier = pltpu.get_barrier_semaphore()

        def greet(step, carry):
            pl.semaphore_signal(barrier, inc=1, device_id=self.z_peer(step), device_id_type=MESH)
            return carry

        lax.fori_loop(1, self.outer, greet, 0)
        for peer in (self.x_peer, self.y_peer, self.diag_peer, self.c_peer):
            pl.semaphore_signal(barrier, inc=1, device_id=peer, device_id_type=MESH)
        pl.semaphore_wait(barrier, self.outer + 3)


def columns(piece, width):
    start = piece * width
    if not isinstance(start, int):
        start = pl.multiple_of(start, width)
    return pl.ds(start, width)


class Weights:
    def __init__(self, k, w, full, send, recv, width):
        self.k, self.w, self.full, self.send, self.recv, self.width = k, w, full, send, recv, width

    def first(self, p, step):
        k, cols = self.k, columns(p, self.width)
        return remote(
            self.w.at[:, cols],
            self.full.at[k.z, k.x, :, cols],
            self.send.at[0, p],
            self.recv.at[0, p],
            k.z_peer(step),
        )

    def all_first(self, p):
        block = self.full.at[pl.ds(0, self.k.outer - 1), 0, :, columns(p, self.width)]
        return remote(block, block, self.send.at[0, p], self.recv.at[0, p], self.k.x_peer)

    def second(self, p):
        block = self.full.at[:, self.k.x, :, columns(p, self.width)]
        return remote(block, block, self.send.at[1, p], self.recv.at[1, p], self.k.x_peer)

    def start(self, pieces):
        def piece(p, carry):
            def one(step, inner):
                self.first(p, step).start()
                return inner

            return lax.fori_loop(1, self.k.outer, one, carry)

        lax.fori_loop(0, pieces, piece, 0)

    def forward(self, p):
        self.all_first(p).wait_recv()
        self.second(p).start()

    def arrive(self, p):
        self.second(p).wait_recv()

    def drain(self, pieces):
        def piece(p, carry):
            self.all_first(p).wait_send()
            self.second(p).wait_send()
            return carry

        lax.fori_loop(0, pieces, piece, 0)


class Gradients:
    def __init__(self, k, part, near, far, out, send, recv, width):
        self.k, self.part, self.near, self.far, self.out = k, part, near, far, out
        self.send, self.recv, self.width = send, recv, width

    def one(self, p):
        k, cols = self.k, columns(p, self.width)
        return remote(
            self.part.at[:, 1 - k.x, :, cols],
            self.near.at[:, :, cols],
            self.send.at[0, p],
            self.recv.at[0, p],
            k.x_peer,
        )

    def two(self, p, step):
        k, cols = self.k, columns(p, self.width)
        return remote(
            self.part.at[lax.rem(k.z + step, k.outer), k.x, :, cols],
            self.far.at[step - 1, :, cols],
            self.send.at[1, p],
            self.recv.at[1, p],
            k.z_peer(step),
        )

    def all_two(self, p):
        block = self.far.at[:, :, columns(p, self.width)]
        return remote(block, block, self.send.at[1, p], self.recv.at[1, p], self.k.x_peer)

    def start(self, p):
        self.one(p).start()

    def forward(self, p):
        k, cols = self.k, columns(p, self.width)
        self.one(p).wait_recv()
        here = self.part[:, k.x, :, cols].astype(F32)
        self.part[:, k.x, :, cols] = (here + self.near[:, :, cols].astype(F32)).astype(BF16)

        def send(step, carry):
            self.two(p, step).start()
            return carry

        lax.fori_loop(1, k.outer, send, 0)

    def finish(self, p):
        k, cols = self.k, columns(p, self.width)
        self.all_two(p).wait_recv()

        def add(i, total):
            return total + self.far[i, :, cols].astype(F32)

        total = self.part[k.z, k.x, :, cols].astype(F32)
        self.out[:, cols] = lax.fori_loop(0, k.outer - 1, add, total)

    def drain(self, pieces):
        def piece(p, carry):
            self.one(p).wait_send()
            self.all_two(p).wait_send()
            return carry

        lax.fori_loop(0, pieces, piece, 0)


class Spread:
    def __init__(self, k, blocks, send, recv, phase):
        self.k, self.blocks, self.send, self.recv, self.phase = k, blocks, send, recv, phase

    def copy(self, number, block, peer):
        ref = self.blocks.at[block]
        return remote(
            ref, ref, self.send.at[self.phase, number], self.recv.at[self.phase, number], peer
        )

    def near(self):
        return self.copy(0, self.k.t, self.k.c_peer)

    def far(self):
        return self.copy(1, self.k.t, self.k.diag_peer)

    def relay(self):
        return self.copy(2, self.k.diag, self.k.c_peer)

    def start(self):
        self.far().start()
        self.near().start()

    def own(self):
        self.near().wait_recv()

    def other(self):
        self.far().wait_recv()
        self.relay().start()
        self.relay().wait_recv()

    def drain(self):
        self.near().wait_send()
        self.far().wait_send()
        self.relay().wait_send()


class Reduce:
    def __init__(self, k, out, inbox, keep, send, recv, phase):
        self.k, self.out, self.inbox, self.keep = k, out, inbox, keep
        self.send, self.recv, self.phase = send, recv, phase

    def copy(self, number, phase=None):
        peer = self.k.y_peer if number == 2 else self.k.c_peer
        phase = self.phase if phase is None else phase
        return remote(
            self.out.at[number],
            self.inbox.at[number],
            self.send.at[phase, number],
            self.recv.at[phase, number],
            peer,
        )

    def free(self, number):
        if self.phase > 0:
            self.copy(number, self.phase - 1).wait_send()

    def across(self, value):
        self.free(0)
        self.out[0] = value.astype(BF16)
        self.copy(0).start()

    def theirs(self, value):
        self.free(2)
        self.copy(0).wait_recv()
        self.out[2] = (value + self.inbox[0].astype(F32)).astype(BF16)
        self.copy(2).start()

    def partner(self, value):
        self.free(1)
        self.out[1] = value.astype(BF16)
        self.copy(1).start()

    def mine(self, value):
        self.keep[...] = value

    def wait(self):
        self.copy(1).wait_recv()
        self.copy(2).wait_recv()

    def total(self, rows):
        return self.keep[rows, :] + (
            self.inbox[1, rows, :].astype(F32) + self.inbox[2, rows, :].astype(F32)
        )

    def drain(self):
        for number in range(3):
            self.copy(number).wait_send()


def fold(values):
    rows, width = values.shape
    return jnp.sum(values.reshape(rows // 8, 8, width), axis=0)


def mean(values):
    return jnp.sum(values, axis=-1, keepdims=True) * (1.0 / values.shape[-1])


def body(
    outer,
    x_ref,
    teacher_ref,
    w_ref,
    vec_ref,
    out_ref,
    gin_ref,
    gsh_ref,
    gvec_ref,
    W,
    G,
    near,
    far,
    X,
    H,
    MX,
    GF,
    Q,
    K,
    V,
    C,
    GC,
    DQKV,
    PT,
    SL,
    ACT,
    GU,
    OWN,
    HID,
    N1,
    R1,
    GS,
    SUMS,
    ACC,
    OUTBOX,
    INBOX,
    VA,
    VR,
    VZ,
    w_send,
    w_recv,
    g_send,
    g_recv,
    s_send,
    s_recv,
    r_send,
    r_recv,
    v_send,
    v_recv,
    own_sem,
):
    k = Place(outer)
    model = x_ref.shape[1]
    rows = x_ref.shape[0]
    heads_width = Q.shape[2]
    inner = ACT.shape[2]
    heads = heads_width // HEAD_DIM
    width = heads_width
    up_piece = 4
    down_piece = 4 + inner // width
    pieces = 4 + 2 * (inner // width)
    scale = 1.0 / math.sqrt(HEAD_DIM)
    mine, theirs = k.y, 1 - k.y

    weights = Weights(k, w_ref, W, w_send, w_recv, width)
    grads = Gradients(k, G, near, far, gsh_ref, g_send, g_recv, width)

    def spread(blocks, phase):
        return Spread(k, blocks, s_send, s_recv, phase)

    def reduce(phase):
        return Reduce(k, OUTBOX, INBOX, OWN, r_send, r_recv, phase)

    def matrix(start, size):
        return W[:, :, :, pl.ds(start, size)].reshape(model, size)

    def vector(row):
        return vec_ref[pl.ds(row, 1), :]

    def pair(blocks, seq):
        return blocks[pl.ds(2 * seq, 2)].reshape(2 * rows, model)

    def part_rows(core):
        return pl.ds(pl.multiple_of(core * rows, rows), rows)

    def norm_loop(step):
        def one(i, carry):
            step(pl.ds(pl.multiple_of(i * CHUNK, CHUNK), CHUNK))
            return carry

        lax.fori_loop(0, rows // CHUNK, one, 0)

    own_w = pltpu.make_async_copy(w_ref, W.at[k.z, k.x], own_sem.at[0])
    own_x = pltpu.make_async_copy(x_ref, X.at[k.t], own_sem.at[1])
    own_w.start()
    own_x.start()
    SUMS[...] = jnp.zeros_like(SUMS)
    VA[0] = jnp.zeros_like(VA[0])
    k.enter()
    own_x.wait()
    s0 = spread(X, 0)
    s0.start()
    weights.start(pieces)
    own_w.wait()
    s0.own()
    s0.other()

    weights.forward(0)
    weights.forward(1)
    for p, held in ((0, Q), (1, K), (2, V)):
        weights.arrive(p)
        weights.forward(p + 2)
        for seq in range(2):
            product = dot(X[pl.ds(2 * seq, 2)].reshape(2 * rows, model), matrix(p * width, width), NN)
            if p != 1:
                bias = vec_ref[p // 2 : p // 2 + 1, pl.ds(pl.multiple_of(k.t * width, width), width)]
                product = product + bias
            held[seq] = product.astype(BF16)

    def head_mask(h):
        lane = lax.broadcasted_iota(jnp.int32, (1, width), 1)
        inside = (lane >= h * HEAD_DIM) & (lane < (h + 1) * HEAD_DIM)
        return jnp.where(inside, 1.0, 0.0).astype(BF16)

    def attend(seq):
        ACC[0] = jnp.zeros_like(ACC[0])

        def head(h, carry):
            mask = head_mask(h)
            scores = dot(K[seq], Q[seq] * mask, NT) * scale
            raised = jnp.exp(scores - jnp.max(scores, axis=0, keepdims=True))
            probs = (raised * (1.0 / jnp.sum(raised, axis=0, keepdims=True))).astype(BF16)
            PT[seq, h] = probs
            ACC[0] += dot(probs, V[seq] * mask, TN)
            return carry

        lax.fori_loop(0, heads, head, 0)
        C[seq] = ACC[0].astype(BF16)

    def out_block(seq, core):
        return dot(C[seq, part_rows(core), :], matrix(3 * width, width), NT)

    r0 = reduce(0)
    attend(theirs)
    weights.arrive(3)
    r0.across(out_block(theirs, 1 - k.c))
    r0.theirs(out_block(theirs, k.c))
    weights.forward(5)
    attend(mine)
    r0.partner(out_block(mine, 1 - k.c))
    r0.mine(out_block(mine, k.c))
    weights.forward(6)
    r0.wait()

    def first_norm(r):
        first = x_ref[r, :].astype(F32) + r0.total(r) + vector(2)
        center = first - mean(first)
        scaling = lax.rsqrt(mean(center * center) + EPSILON)
        normed = center * scaling
        hidden = normed * vector(8) + vector(9)
        N1[r, :] = normed
        R1[r, :] = jnp.broadcast_to(scaling, (CHUNK, R1.shape[1]))
        HID[r, :] = hidden
        H[k.t, r, :] = hidden.astype(BF16)

    norm_loop(first_norm)
    s1 = spread(H, 1)
    s1.start()
    weights.forward(7)
    for p in range(4, 8):
        weights.arrive(p)
    s1.own()

    def up(seq):
        def part(n, carry):
            cols = pl.ds(pl.multiple_of(n * width, width), width)
            wide = pl.ds(pl.multiple_of((up_piece + n) * width, width), width)
            upper = dot(pair(H, seq), W[:, :, :, wide].reshape(model, width), NN)
            upper = upper + vec_ref[pl.ds(3 + k.t, 1), cols]
            erf_part = 1.0 + lax.erf(upper * (1.0 / ROOT_TWO))
            ACT[seq, :, cols] = (0.5 * upper * erf_part).astype(BF16)
            SL[seq, :, cols] = 0.5 * erf_part + upper * jnp.exp(-0.5 * upper * upper) * (
                1.0 / ROOT_TWO_PI
            )
            return carry

        lax.fori_loop(0, inner // width, part, 0)

    def down_block(seq, core):
        return dot(ACT[seq, part_rows(core), :], matrix(down_piece * width, inner), NT)

    up(mine)
    weights.forward(8)
    weights.forward(9)
    s1.other()
    up(theirs)
    weights.forward(10)
    weights.forward(11)
    for p in range(8, 12):
        weights.arrive(p)
    r1 = reduce(1)
    r1.across(down_block(theirs, 1 - k.c))
    r1.theirs(down_block(theirs, k.c))
    r1.partner(down_block(mine, 1 - k.c))
    r1.mine(down_block(mine, k.c))
    r1.wait()

    def norm_back(d, gain, normed, scaling):
        e = d * gain
        return scaling * (e - mean(e) - normed * mean(e * normed))

    def second_norm(r):
        second = HID[r, :] + r1.total(r) + vector(7)
        center = second - mean(second)
        scaling = lax.rsqrt(mean(center * center) + EPSILON)
        normed = center * scaling
        result = normed * vector(10) + vector(11)
        out_ref[r, :] = result.astype(BF16)
        diff = result - teacher_ref[r, :].astype(F32)
        grad = norm_back(diff, vector(10), normed, scaling)
        GS[r, :] = grad
        MX[k.t, r, :] = grad.astype(BF16)
        SUMS[0] += fold(grad)
        SUMS[1] += fold(diff * normed)
        SUMS[2] += fold(diff)
        SUMS[3] += fold(diff * diff)

    norm_loop(second_norm)
    s2 = spread(MX, 2)
    s2.start()
    s2.own()

    def back_up(seq):
        def part(n, carry):
            cols = pl.ds(pl.multiple_of(n * width, width), width)
            wide = pl.ds(pl.multiple_of((down_piece + n) * width, width), width)
            grad = dot(pair(MX, seq), W[:, :, :, wide].reshape(model, width), NN)
            grad = (grad * SL[seq, :, cols]).astype(BF16)
            GU[seq, :, cols] = grad
            SUMS[7, :, cols] += fold(grad.astype(F32))
            return carry

        lax.fori_loop(0, inner // width, part, 0)

    def hidden_block(seq, core):
        return dot(GU[seq, part_rows(core), :], matrix(up_piece * width, inner), NT)

    def weight_grad(left, right, first, count):
        def piece(n, carry):
            cols = pl.ds(pl.multiple_of(n * width, width), width)
            tokens = 4 * rows
            grad = dot(
                left[...].reshape(tokens, model), right[:, :, cols].reshape(tokens, width), TN
            )
            wide = pl.ds(pl.multiple_of((first + n) * width, width), width)
            G[:, :, :, wide] = grad.astype(BF16).reshape(outer, 2, model // (2 * outer), width)

            @pl.when(n > 0)
            def _():
                grads.start(first + n - 1)

            return carry

        lax.fori_loop(0, count, piece, 0)

    r2 = reduce(2)
    back_up(mine)
    s2.other()
    back_up(theirs)
    r2.across(hidden_block(theirs, 1 - k.c))
    r2.theirs(hidden_block(theirs, k.c))
    weight_grad(MX, ACT, down_piece, inner // width)
    r2.partner(hidden_block(mine, 1 - k.c))
    grads.start(down_piece + inner // width - 1)
    r2.mine(hidden_block(mine, k.c))
    weight_grad(H, GU, up_piece, inner // width)
    r2.wait()
    grads.start(up_piece + inner // width - 1)

    def first_back(r):
        grad_hidden = GS[r, :] + r2.total(r)
        normed = N1[r, :]
        grad = norm_back(grad_hidden, vector(8), normed, R1[r, :][:, :1])
        GS[r, :] = grad
        GF[k.t, r, :] = grad.astype(BF16)
        SUMS[4] += fold(grad)
        SUMS[5] += fold(grad_hidden * normed)
        SUMS[6] += fold(grad_hidden)

    norm_loop(first_back)
    s3 = spread(GF, 3)
    s3.start()
    for p in range(8, 12):
        grads.forward(p)
    s3.own()

    def attend_back(seq):
        GC[...] = dot(pair(GF, seq), matrix(3 * width, width), NN).astype(BF16)
        ACC[...] = jnp.zeros_like(ACC)

        def head(h, carry):
            mask = head_mask(h)
            context = GC[...] * mask
            low = PT[seq, h]
            ACC[2] += dot(low, context, NN)
            probs = low.astype(F32)
            grad = dot(V[seq], context, NT)
            across = jnp.sum(probs * grad, axis=0, keepdims=True)
            grad = (probs * (grad - across)).astype(BF16)
            ACC[1] += dot(grad, Q[seq] * mask, NN)
            ACC[0] += dot(grad, K[seq] * mask, TN)
            return carry

        lax.fori_loop(0, heads, head, 0)
        for n in range(3):
            grad = ACC[n] if n == 2 else ACC[n] * scale
            DQKV[seq, :, n * width : (n + 1) * width] = grad.astype(BF16)

    def input_block(seq, core):
        return dot(DQKV[seq, part_rows(core), :], matrix(0, 3 * width), NT)

    attend_back(mine)
    s3.other()
    for p in range(4, 8):
        grads.forward(p)
    attend_back(theirs)
    weight_grad(X, DQKV, 0, 3)
    r3 = reduce(3)
    r3.across(input_block(theirs, 1 - k.c))
    grads.start(2)
    r3.theirs(input_block(theirs, k.c))
    weight_grad(GF, C, 3, 1)
    r3.partner(input_block(mine, 1 - k.c))
    grads.start(3)
    r3.mine(input_block(mine, k.c))

    here = pl.ds(pl.multiple_of(k.t * width, width), width)
    for row, n in ((0, 0), (1, 2)):
        grad = DQKV[:, :, n * width : (n + 1) * width].reshape(4 * rows, width).astype(F32)
        VA[0, row : row + 1, here] = jnp.sum(grad, axis=0, keepdims=True)
    VA[0, pl.ds(3 + k.t, 1), :] = jnp.sum(SUMS[7], axis=0, keepdims=True)
    for row, n in ((7, 0), (10, 1), (11, 2), (12, 3), (2, 4), (8, 5), (9, 6)):
        VA[0, row : row + 1, :] = jnp.sum(SUMS[n], axis=0, keepdims=True)

    def vector_hop(n, peer):
        return remote(VA.at[n], VR.at[n], v_send.at[n], v_recv.at[n], peer)

    def vector_last(step):
        return remote(VA.at[3], VZ.at[k.z], v_send.at[3], v_recv.at[3], k.z_peer(step))

    hops = [vector_hop(n, peer) for n, peer in enumerate((k.c_peer, k.y_peer, k.x_peer))]
    grads.forward(0)
    for n, hop in enumerate(hops):
        hop.start()
        if n < 2:
            grads.forward(1 + n)
        hop.wait_recv()
        VA[n + 1] = VA[n] + VR[n]
    VZ[k.z] = VA[3]
    for p in (3,):
        grads.forward(p)

    def send_last(step, carry):
        vector_last(step).start()
        return carry

    lax.fori_loop(1, outer, send_last, 0)
    for p in (8, 9, 10, 11, 4, 5, 6, 7):
        grads.finish(p)
    r3.wait()

    def last(r):
        gin_ref[r, :] = GS[r, :] + r3.total(r)

    norm_loop(last)
    vz_all = VZ.at[pl.ds(0, outer - 1)]
    every = remote(vz_all, vz_all, v_send.at[3], v_recv.at[3], k.x_peer)
    every.wait_recv()

    def add(i, total):
        return total + VZ[i]

    gvec_ref[...] = lax.fori_loop(1, outer, add, VZ[0])
    for p in (0, 1, 2, 3):
        grads.finish(p)

    weights.drain(pieces)
    grads.drain(pieces)
    for s in (s0, s1, s2, s3):
        s.drain()
    r3.drain()
    for hop in hops:
        hop.wait_send()
    every.wait_send()


def layer(inputs, teacher, w, vec, outer, inner):
    rows, model = inputs.shape
    shard_rows, columns_all = w.shape
    width = (columns_all - 2 * inner) // 4
    heads = width // HEAD_DIM
    pieces = columns_all // width
    seq = 2 * rows
    vmem = pl.BlockSpec(memory_space=pltpu.VMEM)
    full = (outer, 2, shard_rows, columns_all)
    dma = pltpu.SemaphoreType.DMA
    return pl.pallas_call(
        functools.partial(body, outer),
        out_shape=(
            jax.ShapeDtypeStruct((rows, model), BF16),
            jax.ShapeDtypeStruct((rows, model), F32),
            jax.ShapeDtypeStruct((shard_rows, columns_all), F32),
            jax.ShapeDtypeStruct((VECTORS, model), F32),
        ),
        in_specs=[vmem] * 4,
        out_specs=(vmem,) * 4,
        scratch_shapes=[
            pltpu.VMEM(full, BF16),
            pltpu.VMEM(full, BF16),
            pltpu.VMEM((outer, shard_rows, columns_all), BF16),
            pltpu.VMEM((outer - 1, shard_rows, columns_all), BF16),
            pltpu.VMEM((4, rows, model), BF16),
            pltpu.VMEM((4, rows, model), BF16),
            pltpu.VMEM((4, rows, model), BF16),
            pltpu.VMEM((4, rows, model), BF16),
            pltpu.VMEM((2, seq, width), BF16),
            pltpu.VMEM((2, seq, width), BF16),
            pltpu.VMEM((2, seq, width), BF16),
            pltpu.VMEM((2, seq, width), BF16),
            pltpu.VMEM((seq, width), BF16),
            pltpu.VMEM((2, seq, 3 * width), BF16),
            pltpu.VMEM((2, heads, seq, seq), BF16),
            pltpu.VMEM((2, seq, inner), F32),
            pltpu.VMEM((2, seq, inner), BF16),
            pltpu.VMEM((2, seq, inner), BF16),
            pltpu.VMEM((rows, model), F32),
            pltpu.VMEM((rows, model), F32),
            pltpu.VMEM((rows, model), F32),
            pltpu.VMEM((rows, 128), F32),
            pltpu.VMEM((rows, model), F32),
            pltpu.VMEM((8, 8, model), F32),
            pltpu.VMEM((3, seq, width), F32),
            pltpu.VMEM((3, rows, model), BF16),
            pltpu.VMEM((3, rows, model), BF16),
            pltpu.VMEM((4, VECTORS, model), F32),
            pltpu.VMEM((3, VECTORS, model), F32),
            pltpu.VMEM((outer, VECTORS, model), F32),
            dma((2, pieces)),
            dma((2, pieces)),
            dma((2, pieces)),
            dma((2, pieces)),
            dma((4, 3)),
            dma((4, 3)),
            dma((4, 3)),
            dma((4, 3)),
            dma((4,)),
            dma((4,)),
            dma((2,)),
        ],
        compiler_params=pltpu.CompilerParams(
            collective_id=0, has_side_effects=True, vmem_limit_bytes=67043328
        ),
        name="layer",
    )(inputs, teacher, w, vec)


def shards(
    inputs,
    teacher,
    query_weight,
    key_weight,
    value_weight,
    out_weight,
    up_weight,
    down_weight,
    query_bias,
    value_bias,
    out_bias,
    up_bias,
    down_bias,
    first_gain,
    first_shift,
    second_gain,
    second_shift,
):
    local_rows, model = inputs.shape
    width = query_weight.shape[1]
    inner = up_weight.shape[1]
    outer = lax.axis_size("dp") // 2
    w = jnp.concatenate(
        [query_weight, key_weight, value_weight, out_weight.T, up_weight, down_weight.T], axis=1
    )
    vec = jnp.concatenate(
        [
            query_bias,
            value_bias,
            out_bias,
            up_bias,
            down_bias,
            first_gain,
            first_shift,
            second_gain,
            second_shift,
            jnp.zeros(((VECTORS - 12) * model,), F32),
        ]
    ).reshape(VECTORS, model)
    output, grad_inputs, shard, sums = layer(inputs, teacher, w, vec, outer, inner)
    token_total = local_rows * lax.axis_size("dp") * lax.axis_size("tensor")
    loss = 0.5 * jnp.sum(sums[12]) / token_total
    return (
        output,
        loss,
        grad_inputs,
        shard[:, :width],
        shard[:, width : 2 * width],
        shard[:, 2 * width : 3 * width],
        shard[:, 3 * width : 4 * width].T,
        shard[:, 4 * width : 4 * width + inner],
        shard[:, 4 * width + inner :].T,
        sums[0],
        sums[1],
        sums[2],
        sums[3:7].reshape(-1),
        sums[7],
        sums[8],
        sums[9],
        sums[10],
        sums[11],
    )


def solution(mesh):
    tokens = P(("dp", "tensor"), None)
    across, down = P("dp", "tensor"), P("tensor", "dp")
    in_specs = (tokens, tokens, across, across, across, down, across, down) + (P(),) * 9
    out_specs = (tokens, P(), tokens, across, across, across, down, across, down) + (P(),) * 9
    return jax.shard_map(shards, mesh=mesh, in_specs=in_specs, out_specs=out_specs, check_vma=False)
```

time: 945 us -> 268 us (0.28)
  waiting for transfers between devices: 608 us -> 0 us
  Pallas kernels: 0 us -> 238 us
  blocking collectives: 170 us -> 0 us
  matrix products: 78.1 us -> 0 us
  other arithmetic: 24.3 us -> 2.31 us
  between operations: 18.8 us -> 2.48 us
  local copies, waits for them, and re-layouts: 35.1 us -> 24.3 us
    reduce_scatter x10 -> x0, waiting for transfers between devices: 480 us -> none  [the longest x1 91.9 us: shards(): lax.psum_scatter(grad_up, 'dp', scatter_dimension=0, tiled=True)]
    pallas_call x0 -> x1, Pallas kernels: none -> 238 us  [layer(): pl.pallas_call(functools.partial(body, outer), out_shape=(jax.ShapeDtypeS...]
    all_gather x4 -> x0, blocking collectives: 129 us -> none  [the longest x1 35.4 us: shards(): lax.all_gather(query_weight, 'dp', axis=0, tiled=True)]
    all_gather x6 -> x0, waiting for transfers between devices: 127 us -> none  [the longest x1 45 us: shards(): lax.all_gather(down_weight, 'dp', axis=1, tiled=True)]
    dot_general x24 -> x0, matrix products: 78.1 us -> none  [the longest x1 7.37 us: shards(): jnp.dot(spread, full_up, preferred_element_type=jnp.float32) + bias_up]
    psum x1 -> x0, blocking collectives: 40.9 us -> none  [shards(): lax.psum((loss_part, placed(sum_query_bias, model_width, slot * head_widt...]
    reshape x8 -> x1, local copies, waits for them, and re-layouts: 13.6 us -> 0.65 us  [shards(): vec = jnp.concatenate([query_bias, value_bias, out_bias, up_bias, down_bi...]
    reduce_sum x8 -> x0, other arithmetic: 12.4 us -> none  [the longest x2 2.94 us: layer_norm(): center = values - jnp.mean(values, axis=-1, keepdims=True)]
  transfers between devices with their start and end apart: 16 -> 0, of which waited for: 14 -> 0; matrix products, arithmetic and copies ran while one was open for 7% -> 0% of each run, Pallas kernels for 0% -> 0%
where the time goes in v1:
time: 268 us; the launch traced here: 267 us
  Pallas kernels  238 us (89%)
  local copies, waits for them, and re-layouts  24.3 us (9%)
    pallas_call x1, Pallas kernels, layer(): pl.pallas_call(functools.partial(body, outer), out_shape=(jax.ShapeDtypeS...  238 us
    unnamed x28, local copies, waits for them, and re-layouts  19 us

profile of v1, /device:TPU:0, one launch (start us, length us, event | category | flops | bytes accessed | tf_op | source)
XLA Modules:
  0.0 266.7 jit_solution(17984449134707574716)
XLA Ops:
  0.7 0.0 copy-start.2
  0.7 1.0 copy.35
  1.7 0.7 constant_dynamic-update-slice_fusion.4
  2.3 0.7 constant_dynamic-update-slice_fusion.6
  3.0 0.7 constant_dynamic-update-slice_fusion.5
  3.7 0.7 constant_dynamic-update-slice_fusion.12
  4.4 0.7 constant_dynamic-update-slice_fusion.11
  5.1 0.7 constant_dynamic-update-slice_fusion.10
  5.8 0.7 constant_dynamic-update-slice_fusion.9
  6.5 0.7 constant_dynamic-update-slice_fusion.8
  7.2 0.7 constant_dynamic-update-slice_fusion.7
  7.9 0.6 reshape.42.vec_ref
  8.5 1.1 copy.36
  9.6 1.5 constant_dynamic-update-slice_fusion.3
  11.1 1.5 constant_dynamic-update-slice_fusion.2
  12.6 1.5 constant_dynamic-update-slice_fusion.1
  14.0 0.6 bitcast_dynamic-update-slice_fusion.1
  14.7 0.0 copy-done.2
  14.7 0.7 constant_dynamic-update-slice_fusion
  15.4 0.7 bitcast_dynamic-update-slice_fusion.w_ref
  16.1 237.5 %layer.1 = (bf16[256,1024]{1,0:T(8,128)(2,1)}, f32[256,1024]{1,0:T(8,128)}, f32[128,3072]{1,0:T(8,128)}, f32[16,1024]{1,0:T(8,128)}) custom-call(bf16[256,1024]{1,0:T(8,128)(2,1)} %x_ref.1, bf16[256,1024]{1,0:T(8,128)(2,1)} %teacher_ref.1, bf16[128,3072]{1,0:T(8,128)(2,1)} %bitcast_dynamic-update-slice_fusion.w_ref, f32[16,1024]{1,0:T(8,128)} %reshape.42.vec_ref), custom_call_target="tpu_custom_call" | custom-call | tf_op jit(solution)/shard_map/layer/pallas_call | solution.py:689
  253.7 0.8 slice_bitcast_fusion.2
  254.4 2.3 fusion
  257.4 0.6 copy.41
  258.0 1.8 slice_bitcast_fusion.1
  259.9 0.0 copy-start.1
  259.9 2.1 slice_bitcast_fusion
  262.0 0.0 copy-start
  262.0 1.0 copy.38
  263.0 0.8 copy.37
  263.7 0.0 copy-done.1
  263.8 0.8 copy.58
  264.5 0.0 copy-done
  264.5 1.0 copy.59
  (1 shorter events, 0.0 us)
Async XLA Ops:
  0.7 14.0 %copy-start.2 = (bf16[128,1024]{1,0:T(8,128)(2,1)S(1)}, bf16[128,1024]{1,0:T(8,128)(2,1)}, u32[]{:S(2)}) copy-start(bf16[128,1024]{1,0:T(8,128)(2,1)} %param.23) | copy-start | bytes 786436
  259.9 3.9 %copy-start.1 = (bf16[256,1024]{1,0:T(8,128)(2,1)S(1)}, bf16[256,1024]{1,0:T(8,128)(2,1)}, u32[]{:S(2)}) copy-start(bf16[256,1024]{1,0:T(8,128)(2,1)} %get-tuple-element.77) | copy-start | bytes 1572868
  262.0 2.5 copy-start

commit v2 on v1

--- a/solution.py
+++ b/solution.py
@@ -18,6 +18,7 @@
 NT = ((1,), (1,))
 TN = ((0,), (0,))
 CHUNK = 32
+WINDOW = 3
 ROOT_TWO = math.sqrt(2.0)
 ROOT_TWO_PI = math.sqrt(2.0 * math.pi)
 VECTORS = 16
@@ -49,17 +50,19 @@
     def z_peer(self, step):
         return (lax.rem(self.z + step, self.outer) * 2 + self.x, self.t)
 
-    def enter(self):
+    def greet(self):
         barrier = pltpu.get_barrier_semaphore()
 
-        def greet(step, carry):
+        def one(step, carry):
             pl.semaphore_signal(barrier, inc=1, device_id=self.z_peer(step), device_id_type=MESH)
             return carry
 
-        lax.fori_loop(1, self.outer, greet, 0)
+        lax.fori_loop(1, self.outer, one, 0)
         for peer in (self.x_peer, self.y_peer, self.diag_peer, self.c_peer):
             pl.semaphore_signal(barrier, inc=1, device_id=peer, device_id_type=MESH)
-        pl.semaphore_wait(barrier, self.outer + 3)
+
+    def enter(self):
+        pl.semaphore_wait(pltpu.get_barrier_semaphore(), self.outer + 3)
 
 
 def columns(piece, width):
@@ -70,18 +73,13 @@
 
 
 class Weights:
-    def __init__(self, k, w, full, send, recv, width):
-        self.k, self.w, self.full, self.send, self.recv, self.width = k, w, full, send, recv, width
+    def __init__(self, k, full, send, recv, width, pieces):
+        self.k, self.full, self.send, self.recv, self.width = k, full, send, recv, width
+        self.pieces = pieces
 
     def first(self, p, step):
-        k, cols = self.k, columns(p, self.width)
-        return remote(
-            self.w.at[:, cols],
-            self.full.at[k.z, k.x, :, cols],
-            self.send.at[0, p],
-            self.recv.at[0, p],
-            k.z_peer(step),
-        )
+        block = self.full.at[self.k.z, self.k.x, :, columns(p, self.width)]
+        return remote(block, block, self.send.at[0, p], self.recv.at[0, p], self.k.z_peer(step))
 
     def all_first(self, p):
         block = self.full.at[pl.ds(0, self.k.outer - 1), 0, :, columns(p, self.width)]
@@ -91,19 +89,18 @@
         block = self.full.at[:, self.k.x, :, columns(p, self.width)]
         return remote(block, block, self.send.at[1, p], self.recv.at[1, p], self.k.x_peer)
 
-    def start(self, pieces):
-        def piece(p, carry):
-            def one(step, inner):
-                self.first(p, step).start()
-                return inner
-
-            return lax.fori_loop(1, self.k.outer, one, carry)
-
-        lax.fori_loop(0, pieces, piece, 0)
+    def start(self, p):
+        def one(step, carry):
+            self.first(p, step).start()
+            return carry
+
+        lax.fori_loop(1, self.k.outer, one, 0)
 
     def forward(self, p):
         self.all_first(p).wait_recv()
         self.second(p).start()
+        if p + WINDOW < self.pieces:
+            self.start(p + WINDOW)
 
     def arrive(self, p):
         self.second(p).wait_recv()
@@ -169,7 +166,8 @@
             return total + self.far[i, :, cols].astype(F32)
 
         total = self.part[k.z, k.x, :, cols].astype(F32)
-        self.out[:, cols] = lax.fori_loop(0, k.outer - 1, add, total)
+        total = lax.fori_loop(0, k.outer - 1, add, total)
+        self.out(p, total)
 
     def drain(self, pieces):
         def piece(p, carry):
@@ -206,9 +204,11 @@
     def own(self):
         self.near().wait_recv()
 
-    def other(self):
+    def pass_on(self):
         self.far().wait_recv()
         self.relay().start()
+
+    def other(self):
         self.relay().wait_recv()
 
     def drain(self):
@@ -281,13 +281,31 @@
 
 def body(
     outer,
-    x_ref,
-    teacher_ref,
-    w_ref,
-    vec_ref,
+    x_in,
+    teacher_in,
+    qw_in,
+    kw_in,
+    vw_in,
+    ow_in,
+    uw_in,
+    dw_in,
+    qb_in,
+    vb_in,
+    ob_in,
+    ub_in,
+    db_in,
+    g1_in,
+    b1_in,
+    g2_in,
+    b2_in,
     out_ref,
     gin_ref,
-    gsh_ref,
+    gq_ref,
+    gk_ref,
+    gv_ref,
+    go_ref,
+    gu_ref,
+    gd_ref,
     gvec_ref,
     W,
     G,
@@ -319,6 +337,10 @@
     VA,
     VR,
     VZ,
+    TEACH,
+    OT,
+    DT,
+    VEC,
     w_send,
     w_recv,
     g_send,
@@ -329,23 +351,54 @@
     r_recv,
     v_send,
     v_recv,
-    own_sem,
+    load_sem,
 ):
     k = Place(outer)
-    model = x_ref.shape[1]
-    rows = x_ref.shape[0]
-    heads_width = Q.shape[2]
+    rows, model = x_in.shape
+    width = Q.shape[2]
     inner = ACT.shape[2]
-    heads = heads_width // HEAD_DIM
-    width = heads_width
+    heads = width // HEAD_DIM
+    steps = inner // width
     up_piece = 4
-    down_piece = 4 + inner // width
-    pieces = 4 + 2 * (inner // width)
+    down_piece = 4 + steps
+    pieces = 4 + 2 * steps
     scale = 1.0 / math.sqrt(HEAD_DIM)
     mine, theirs = k.y, 1 - k.y
 
-    weights = Weights(k, w_ref, W, w_send, w_recv, width)
-    grads = Gradients(k, G, near, far, gsh_ref, g_send, g_recv, width)
+    own = W.at[k.z, k.x]
+    loads = []
+
+    def load(src, dst):
+        copy = pltpu.make_async_copy(src, dst, load_sem.at[len(loads)])
+        copy.start()
+        loads.append(copy)
+
+    load(x_in, X.at[k.t])
+    load(qw_in, own.at[:, columns(0, width)])
+    load(kw_in, own.at[:, columns(1, width)])
+    load(vw_in, own.at[:, columns(2, width)])
+    load(ow_in, OT)
+    load(uw_in, own.at[:, pl.ds(4 * width, inner)])
+    load(dw_in, DT)
+    load(teacher_in, TEACH)
+    for row, ref in enumerate((qb_in, vb_in, ob_in, db_in, g1_in, b1_in, g2_in, b2_in)):
+        load(ref, VEC.at[pl.ds(row, 1), pl.ds(0, model)])
+    load(ub_in, VEC.at[pl.ds(8, 1), :])
+    k.greet()
+
+    weights = Weights(k, W, w_send, w_recv, width, pieces)
+
+    def keep(p, total):
+        if p < 3:
+            (gq_ref, gk_ref, gv_ref)[p][...] = total
+        elif p == 3:
+            go_ref[...] = total.T
+        elif p < down_piece:
+            gu_ref[:, (p - up_piece) * width : (p - up_piece + 1) * width] = total
+        else:
+            gd_ref[(p - down_piece) * width : (p - down_piece + 1) * width, :] = total.T
+
+    grads = Gradients(k, G, near, far, keep, g_send, g_recv, width)
 
     def spread(blocks, phase):
         return Spread(k, blocks, s_send, s_recv, phase)
@@ -357,7 +410,7 @@
         return W[:, :, :, pl.ds(start, size)].reshape(model, size)
 
     def vector(row):
-        return vec_ref[pl.ds(row, 1), :]
+        return VEC[row : row + 1, 0:model]
 
     def pair(blocks, seq):
         return blocks[pl.ds(2 * seq, 2)].reshape(2 * rows, model)
@@ -372,31 +425,26 @@
 
         lax.fori_loop(0, rows // CHUNK, one, 0)
 
-    own_w = pltpu.make_async_copy(w_ref, W.at[k.z, k.x], own_sem.at[0])
-    own_x = pltpu.make_async_copy(x_ref, X.at[k.t], own_sem.at[1])
-    own_w.start()
-    own_x.start()
     SUMS[...] = jnp.zeros_like(SUMS)
     VA[0] = jnp.zeros_like(VA[0])
+    for copy in loads:
+        copy.wait()
+    own[:, columns(3, width)] = OT[...].T
+    own[:, pl.ds(4 * width + inner, inner)] = DT[...].T
+    s0 = spread(X, 0)
     k.enter()
-    own_x.wait()
-    s0 = spread(X, 0)
     s0.start()
-    weights.start(pieces)
-    own_w.wait()
-    s0.own()
-    s0.other()
-
-    weights.forward(0)
-    weights.forward(1)
-    for p, held in ((0, Q), (1, K), (2, V)):
+    for p in range(WINDOW):
+        weights.start(p)
+
+    def project(p, held):
         weights.arrive(p)
-        weights.forward(p + 2)
         for seq in range(2):
-            product = dot(X[pl.ds(2 * seq, 2)].reshape(2 * rows, model), matrix(p * width, width), NN)
+            tokens = X[2 * seq : 2 * seq + 2].reshape(2 * rows, model)
+            product = dot(tokens, matrix(p * width, width), NN)
             if p != 1:
-                bias = vec_ref[p // 2 : p // 2 + 1, pl.ds(pl.multiple_of(k.t * width, width), width)]
-                product = product + bias
+                here = pl.ds(pl.multiple_of(k.t * width, width), width)
+                product = product + VEC[p // 2 : p // 2 + 1, here]
             held[seq] = product.astype(BF16)
 
     def head_mask(h):
@@ -422,24 +470,35 @@
     def out_block(seq, core):
         return dot(C[seq, part_rows(core), :], matrix(3 * width, width), NT)
 
+    weights.forward(0)
+    weights.forward(1)
+    s0.pass_on()
+    s0.own()
+    s0.other()
+    project(0, Q)
+    weights.forward(2)
+    project(1, K)
+    weights.forward(3)
+    project(2, V)
     r0 = reduce(0)
     attend(theirs)
+    weights.forward(4)
     weights.arrive(3)
     r0.across(out_block(theirs, 1 - k.c))
     r0.theirs(out_block(theirs, k.c))
+    attend(mine)
     weights.forward(5)
-    attend(mine)
     r0.partner(out_block(mine, 1 - k.c))
     r0.mine(out_block(mine, k.c))
     weights.forward(6)
     r0.wait()
 
     def first_norm(r):
-        first = x_ref[r, :].astype(F32) + r0.total(r) + vector(2)
+        first = X[k.t, r, :].astype(F32) + r0.total(r) + vector(2)
         center = first - mean(first)
         scaling = lax.rsqrt(mean(center * center) + EPSILON)
         normed = center * scaling
-        hidden = normed * vector(8) + vector(9)
+        hidden = normed * vector(4) + vector(5)
         N1[r, :] = normed
         R1[r, :] = jnp.broadcast_to(scaling, (CHUNK, R1.shape[1]))
         HID[r, :] = hidden
@@ -449,16 +508,17 @@
     s1 = spread(H, 1)
     s1.start()
     weights.forward(7)
-    for p in range(4, 8):
+    weights.forward(8)
+    s1.own()
+    for p in range(up_piece, down_piece):
         weights.arrive(p)
-    s1.own()
 
     def up(seq):
         def part(n, carry):
             cols = pl.ds(pl.multiple_of(n * width, width), width)
             wide = pl.ds(pl.multiple_of((up_piece + n) * width, width), width)
             upper = dot(pair(H, seq), W[:, :, :, wide].reshape(model, width), NN)
-            upper = upper + vec_ref[pl.ds(3 + k.t, 1), cols]
+            upper = upper + VEC[8:9, pl.ds(pl.multiple_of(k.t * inner + n * width, width), width)]
             erf_part = 1.0 + lax.erf(upper * (1.0 / ROOT_TWO))
             ACT[seq, :, cols] = (0.5 * upper * erf_part).astype(BF16)
             SL[seq, :, cols] = 0.5 * erf_part + upper * jnp.exp(-0.5 * upper * upper) * (
@@ -466,19 +526,19 @@
             )
             return carry
 
-        lax.fori_loop(0, inner // width, part, 0)
+        lax.fori_loop(0, steps, part, 0)
 
     def down_block(seq, core):
         return dot(ACT[seq, part_rows(core), :], matrix(down_piece * width, inner), NT)
 
     up(mine)
-    weights.forward(8)
     weights.forward(9)
+    s1.pass_on()
     s1.other()
     up(theirs)
     weights.forward(10)
     weights.forward(11)
-    for p in range(8, 12):
+    for p in range(down_piece, pieces):
         weights.arrive(p)
     r1 = reduce(1)
     r1.across(down_block(theirs, 1 - k.c))
@@ -492,14 +552,14 @@
         return scaling * (e - mean(e) - normed * mean(e * normed))
 
     def second_norm(r):
-        second = HID[r, :] + r1.total(r) + vector(7)
+        second = HID[r, :] + r1.total(r) + vector(3)
         center = second - mean(second)
         scaling = lax.rsqrt(mean(center * center) + EPSILON)
         normed = center * scaling
-        result = normed * vector(10) + vector(11)
+        result = normed * vector(6) + vector(7)
         out_ref[r, :] = result.astype(BF16)
-        diff = result - teacher_ref[r, :].astype(F32)
-        grad = norm_back(diff, vector(10), normed, scaling)
+        diff = result - TEACH[r, :].astype(F32)
+        grad = norm_back(diff, vector(6), normed, scaling)
         GS[r, :] = grad
         MX[k.t, r, :] = grad.astype(BF16)
         SUMS[0] += fold(grad)
@@ -522,12 +582,12 @@
             SUMS[7, :, cols] += fold(grad.astype(F32))
             return carry
 
-        lax.fori_loop(0, inner // width, part, 0)
+        lax.fori_loop(0, steps, part, 0)
 
     def hidden_block(seq, core):
         return dot(GU[seq, part_rows(core), :], matrix(up_piece * width, inner), NT)
 
-    def weight_grad(left, right, first, count):
+    def weight_grad(left, right, first, begin, end):
         def piece(n, carry):
             cols = pl.ds(pl.multiple_of(n * width, width), width)
             tokens = 4 * rows
@@ -537,32 +597,38 @@
             wide = pl.ds(pl.multiple_of((first + n) * width, width), width)
             G[:, :, :, wide] = grad.astype(BF16).reshape(outer, 2, model // (2 * outer), width)
 
-            @pl.when(n > 0)
+            @pl.when(n > begin)
             def _():
                 grads.start(first + n - 1)
 
             return carry
 
-        lax.fori_loop(0, count, piece, 0)
+        lax.fori_loop(begin, end, piece, 0)
 
     r2 = reduce(2)
     back_up(mine)
+    r2.partner(hidden_block(mine, 1 - k.c))
+    r2.mine(hidden_block(mine, k.c))
+    s2.pass_on()
     s2.other()
+    weight_grad(MX, ACT, down_piece, 0, 2)
     back_up(theirs)
+    grads.start(down_piece + 1)
     r2.across(hidden_block(theirs, 1 - k.c))
     r2.theirs(hidden_block(theirs, k.c))
-    weight_grad(MX, ACT, down_piece, inner // width)
-    r2.partner(hidden_block(mine, 1 - k.c))
-    grads.start(down_piece + inner // width - 1)
-    r2.mine(hidden_block(mine, k.c))
-    weight_grad(H, GU, up_piece, inner // width)
+    weight_grad(MX, ACT, down_piece, 2, steps)
+    grads.forward(8)
+    grads.start(down_piece + steps - 1)
+    weight_grad(H, GU, up_piece, 0, steps)
+    grads.start(up_piece + steps - 1)
+    grads.forward(9)
+    grads.forward(10)
     r2.wait()
-    grads.start(up_piece + inner // width - 1)
 
     def first_back(r):
         grad_hidden = GS[r, :] + r2.total(r)
         normed = N1[r, :]
-        grad = norm_back(grad_hidden, vector(8), normed, R1[r, :][:, :1])
+        grad = norm_back(grad_hidden, vector(4), normed, R1[r, :][:, :1])
         GS[r, :] = grad
         GF[k.t, r, :] = grad.astype(BF16)
         SUMS[4] += fold(grad)
@@ -572,8 +638,6 @@
     norm_loop(first_back)
     s3 = spread(GF, 3)
     s3.start()
-    for p in range(8, 12):
-        grads.forward(p)
     s3.own()
 
     def attend_back(seq):
@@ -602,19 +666,14 @@
         return dot(DQKV[seq, part_rows(core), :], matrix(0, 3 * width), NT)
 
     attend_back(mine)
+    grads.forward(11)
+    s3.pass_on()
+    grads.forward(4)
     s3.other()
-    for p in range(4, 8):
-        grads.forward(p)
+    weight_grad(GF, C, 3, 0, 1)
+    grads.forward(5)
     attend_back(theirs)
-    weight_grad(X, DQKV, 0, 3)
-    r3 = reduce(3)
-    r3.across(input_block(theirs, 1 - k.c))
-    grads.start(2)
-    r3.theirs(input_block(theirs, k.c))
-    weight_grad(GF, C, 3, 1)
-    r3.partner(input_block(mine, 1 - k.c))
     grads.start(3)
-    r3.mine(input_block(mine, k.c))
 
     here = pl.ds(pl.multiple_of(k.t * width, width), width)
     for row, n in ((0, 0), (1, 2)):
@@ -631,30 +690,51 @@
         return remote(VA.at[3], VZ.at[k.z], v_send.at[3], v_recv.at[3], k.z_peer(step))
 
     hops = [vector_hop(n, peer) for n, peer in enumerate((k.c_peer, k.y_peer, k.x_peer))]
+
+    def hop_in(n):
+        hops[n].wait_recv()
+        VA[n + 1] = VA[n] + VR[n]
+
+    weight_grad(X, DQKV, 0, 0, 1)
+    hops[0].start()
+    weight_grad(X, DQKV, 0, 1, 2)
+    grads.start(0)
+    hop_in(0)
+    hops[1].start()
+    weight_grad(X, DQKV, 0, 2, 3)
+    grads.start(1)
+    grads.forward(6)
+    r3 = reduce(3)
+    r3.across(input_block(theirs, 1 - k.c))
+    r3.theirs(input_block(theirs, k.c))
+    hop_in(1)
+    hops[2].start()
+    grads.start(2)
+    grads.forward(7)
+    r3.partner(input_block(mine, 1 - k.c))
+    r3.mine(input_block(mine, k.c))
+    for p in (8, 9, 10):
+        grads.finish(p)
+    grads.forward(3)
     grads.forward(0)
-    for n, hop in enumerate(hops):
-        hop.start()
-        if n < 2:
-            grads.forward(1 + n)
-        hop.wait_recv()
-        VA[n + 1] = VA[n] + VR[n]
+    grads.forward(1)
+    hop_in(2)
     VZ[k.z] = VA[3]
-    for p in (3,):
-        grads.forward(p)
 
     def send_last(step, carry):
         vector_last(step).start()
         return carry
 
     lax.fori_loop(1, outer, send_last, 0)
-    for p in (8, 9, 10, 11, 4, 5, 6, 7):
-        grads.finish(p)
+    grads.forward(2)
     r3.wait()
 
     def last(r):
         gin_ref[r, :] = GS[r, :] + r3.total(r)
 
     norm_loop(last)
+    for p in (11, 4, 5, 6, 7, 3, 0, 1):
+        grads.finish(p)
     vz_all = VZ.at[pl.ds(0, outer - 1)]
     every = remote(vz_all, vz_all, v_send.at[3], v_recv.at[3], k.x_peer)
     every.wait_recv()
@@ -663,8 +743,7 @@
         return total + VZ[i]
 
     gvec_ref[...] = lax.fori_loop(1, outer, add, VZ[0])
-    for p in (0, 1, 2, 3):
-        grads.finish(p)
+    grads.finish(2)
 
     weights.drain(pieces)
     grads.drain(pieces)
@@ -676,26 +755,35 @@
     every.wait_send()
 
 
-def layer(inputs, teacher, w, vec, outer, inner):
+def layer(outer, arrays):
+    inputs, query_weight, up_weight = arrays[0], arrays[2], arrays[6]
     rows, model = inputs.shape
-    shard_rows, columns_all = w.shape
-    width = (columns_all - 2 * inner) // 4
+    shard_rows, width = query_weight.shape
+    inner = up_weight.shape[1]
     heads = width // HEAD_DIM
+    columns_all = 4 * width + 2 * inner
     pieces = columns_all // width
     seq = 2 * rows
     vmem = pl.BlockSpec(memory_space=pltpu.VMEM)
+    anywhere = pl.BlockSpec(memory_space=pl.ANY)
     full = (outer, 2, shard_rows, columns_all)
     dma = pltpu.SemaphoreType.DMA
+    outs = (
+        jax.ShapeDtypeStruct((rows, model), BF16),
+        jax.ShapeDtypeStruct((rows, model), F32),
+        jax.ShapeDtypeStruct((shard_rows, width), F32),
+        jax.ShapeDtypeStruct((shard_rows, width), F32),
+        jax.ShapeDtypeStruct((shard_rows, width), F32),
+        jax.ShapeDtypeStruct((width, shard_rows), F32),
+        jax.ShapeDtypeStruct((shard_rows, inner), F32),
+        jax.ShapeDtypeStruct((inner, shard_rows), F32),
+        jax.ShapeDtypeStruct((VECTORS, model), F32),
+    )
     return pl.pallas_call(
         functools.partial(body, outer),
-        out_shape=(
-            jax.ShapeDtypeStruct((rows, model), BF16),
-            jax.ShapeDtypeStruct((rows, model), F32),
-            jax.ShapeDtypeStruct((shard_rows, columns_all), F32),
-            jax.ShapeDtypeStruct((VECTORS, model), F32),
-        ),
-        in_specs=[vmem] * 4,
-        out_specs=(vmem,) * 4,
+        out_shape=outs,
+        in_specs=[anywhere] * len(arrays),
+        out_specs=(vmem,) * len(outs),
         scratch_shapes=[
             pltpu.VMEM(full, BF16),
             pltpu.VMEM(full, BF16),
@@ -727,6 +815,10 @@
             pltpu.VMEM((4, VECTORS, model), F32),
             pltpu.VMEM((3, VECTORS, model), F32),
             pltpu.VMEM((outer, VECTORS, model), F32),
+            pltpu.VMEM((rows, model), BF16),
+            pltpu.VMEM((width, shard_rows), BF16),
+            pltpu.VMEM((inner, shard_rows), BF16),
+            pltpu.VMEM((9, 4 * inner), F32),
             dma((2, pieces)),
             dma((2, pieces)),
             dma((2, pieces)),
@@ -737,77 +829,59 @@
             dma((4, 3)),
             dma((4,)),
             dma((4,)),
-            dma((2,)),
+            dma((len(arrays),)),
         ],
         compiler_params=pltpu.CompilerParams(
             collective_id=0, has_side_effects=True, vmem_limit_bytes=67043328
         ),
         name="layer",
-    )(inputs, teacher, w, vec)
-
-
-def shards(
-    inputs,
-    teacher,
-    query_weight,
-    key_weight,
-    value_weight,
-    out_weight,
-    up_weight,
-    down_weight,
-    query_bias,
-    value_bias,
-    out_bias,
-    up_bias,
-    down_bias,
-    first_gain,
-    first_shift,
-    second_gain,
-    second_shift,
-):
-    local_rows, model = inputs.shape
-    width = query_weight.shape[1]
-    inner = up_weight.shape[1]
+    )(*arrays)
+
+
+def write_body(count, *refs):
+    ins, outs, sem = refs[:9], refs[9 : 9 + count], refs[-1]
+    vec = ins[8]
+    pairs = list(zip(ins[:8], outs[:8]))
+    single = [(0, 8), (1, 9), (2, 10), (7, 12), (8, 13), (9, 14), (10, 15), (11, 16), (12, 17)]
+    pairs += [(vec.at[pl.ds(row, 1), :], outs[place]) for row, place in single]
+    model = vec.shape[1]
+    parts = outs[11].shape[1] // model
+    for n in range(parts):
+        pairs.append((vec.at[pl.ds(3 + n, 1), :], outs[11].at[:, pl.ds(n * model, model)]))
+    copies = [pltpu.make_async_copy(src, dst, sem.at[n]) for n, (src, dst) in enumerate(pairs)]
+    for copy in copies:
+        copy.start()
+    for copy in copies:
+        copy.wait()
+
+
+def write(values, up_length):
+    model = values[8].shape[1]
+    line = jax.ShapeDtypeStruct((1, model), F32)
+    outs = [jax.ShapeDtypeStruct(v.shape, v.dtype) for v in values[:8]] + [line] * 10
+    outs[11] = jax.ShapeDtypeStruct((1, up_length), F32)
+    copies = 17 + up_length // model
+    return pl.pallas_call(
+        functools.partial(write_body, len(outs)),
+        out_shape=tuple(outs),
+        in_specs=[pl.BlockSpec(memory_space=pltpu.VMEM)] * len(values),
+        out_specs=(pl.BlockSpec(memory_space=pl.ANY),) * len(outs),
+        scratch_shapes=[pltpu.SemaphoreType.DMA((copies,))],
+        name="write",
+    )(*values)
+
+
+def shards(*arrays):
+    inputs = arrays[0]
     outer = lax.axis_size("dp") // 2
-    w = jnp.concatenate(
-        [query_weight, key_weight, value_weight, out_weight.T, up_weight, down_weight.T], axis=1
-    )
-    vec = jnp.concatenate(
-        [
-            query_bias,
-            value_bias,
-            out_bias,
-            up_bias,
-            down_bias,
-            first_gain,
-            first_shift,
-            second_gain,
-            second_shift,
-            jnp.zeros(((VECTORS - 12) * model,), F32),
-        ]
-    ).reshape(VECTORS, model)
-    output, grad_inputs, shard, sums = layer(inputs, teacher, w, vec, outer, inner)
-    token_total = local_rows * lax.axis_size("dp") * lax.axis_size("tensor")
-    loss = 0.5 * jnp.sum(sums[12]) / token_total
-    return (
-        output,
-        loss,
-        grad_inputs,
-        shard[:, :width],
-        shard[:, width : 2 * width],
-        shard[:, 2 * width : 3 * width],
-        shard[:, 3 * width : 4 * width].T,
-        shard[:, 4 * width : 4 * width + inner],
-        shard[:, 4 * width + inner :].T,
-        sums[0],
-        sums[1],
-        sums[2],
-        sums[3:7].reshape(-1),
-        sums[7],
-        sums[8],
-        sums[9],
-        sums[10],
-        sums[11],
+    arrays = arrays[:8] + tuple(v.reshape(1, -1) for v in arrays[8:])
+    up_length = arrays[11].shape[1]
+    values = write(layer(outer, arrays), up_length)
+    token_total = inputs.shape[0] * lax.axis_size("dp") * lax.axis_size("tensor")
+    loss = jnp.sum(values[17]) * (0.5 / token_total)
+    output, grad_inputs, gq, gk, gv, go, gu, gd = values[:8]
+    return (output, loss, grad_inputs, gq, gk, gv, go, gu, gd) + tuple(
+        v.reshape(-1) for v in values[8:17]
     )
 
 

time: 268 us -> 222 us (0.83)
  local copies, waits for them, and re-layouts: 24.3 us -> 0.65 us
  Pallas kernels: 238 us -> 218 us
    pallas_call x1 -> x2, Pallas kernels: 238 us -> 218 us  [the longest x1 214 us: layer(): pl.pallas_call(functools.partial(body, outer), out_shape=outs, in_specs=[...]
    unnamed x28 -> x2, local copies, waits for them, and re-layouts: 19 us -> 0.65 us
    transpose x2 -> x0, local copies, waits for them, and re-layouts: 3.99 us -> none  [the longest x1 2.14 us: shards(): shard[:, 4 * width + inner:]]
where the time goes in v2:
time: 222 us; the launch traced here: 221 us
  Pallas kernels  218 us (98%)
  between operations  2.46 us (1%)
    pallas_call x1, Pallas kernels, layer(): pl.pallas_call(functools.partial(body, outer), out_shape=outs, in_specs=[...  214 us

profile of v2, /device:TPU:0, one launch (start us, length us, event | category | flops | bytes accessed | tf_op | source)
XLA Modules:
  0.0 221.5 jit_solution(2478775036451461250)
XLA Ops:
  0.7 214.0 %layer.1 = (bf16[256,1024]{1,0:T(8,128)(2,1)}, f32[256,1024]{1,0:T(8,128)}, f32[128,256]{1,0:T(8,128)}, f32[128,256]{1,0:T(8,128)}, f32[128,256]{1,0:T(8,128)}, ...) custom-call(bf16[256,1024]{1,0:T(8,128)(2,1)} %x_in.1, ...), custom_call_target="tpu_custom_call" | custom-call | tf_op jit(solution)/shard_map/layer/pallas_call | solution.py:782
  214.7 3.7 %write.1 = (bf16[256,1024]{1,0:T(8,128)(2,1)}, f32[256,1024]{1,0:T(8,128)}, f32[128,256]{1,0:T(8,128)}, f32[128,256]{1,0:T(8,128)}, f32[128,256]{1,0:T(8,128)}, ...) custom-call(bf16[256,1024]{1,0:T(8,128)(2,1)} %get-tuple-element.45., ...), custom_call_target="tpu_custom_call" | custom-call | tf_op jit(solution)/shard_map/write/pallas_call | solution.py:864
  218.4 0.0 copy-start
  218.4 0.7 copy-done
  219.1 0.6 reduce_sum.9
Async XLA Ops:
  218.4 0.7 copy-start

commit v3 on v2

--- a/solution.py
+++ b/solution.py
@@ -217,6 +217,43 @@
         self.relay().wait_send()
 
 
+class SpreadColumns(Spread):
+    def __init__(self, k, blocks, send, recv, phase, chunks, far_sems):
+        super().__init__(k, blocks, send, recv, phase)
+        self.chunks = chunks
+        self.far_send, self.far_recv, self.relay_send, self.relay_recv = far_sems
+
+    def cols(self, chunk):
+        width = self.blocks.shape[2] // self.chunks
+        return pl.ds(pl.multiple_of(chunk * width, width), width)
+
+    def far_part(self, n, chunk):
+        ref = self.blocks.at[self.k.t, :, self.cols(chunk)]
+        return remote(ref, ref, self.far_send.at[n], self.far_recv.at[n], self.k.diag_peer)
+
+    def relay_part(self, n, chunk):
+        ref = self.blocks.at[self.k.diag, :, self.cols(chunk)]
+        return remote(ref, ref, self.relay_send.at[n], self.relay_recv.at[n], self.k.c_peer)
+
+    def start_columns(self, order):
+        self.near().start()
+        for n, chunk in enumerate(order):
+            self.far_part(n, chunk).start()
+
+    def pass_part(self, n, chunk):
+        self.far_part(n, chunk).wait_recv()
+        self.relay_part(n, chunk).start()
+
+    def other_part(self, n, chunk):
+        self.relay_part(n, chunk).wait_recv()
+
+    def drain_columns(self, order):
+        self.near().wait_send()
+        for n, chunk in enumerate(order):
+            self.far_part(n, chunk).wait_send()
+            self.relay_part(n, chunk).wait_send()
+
+
 class Reduce:
     def __init__(self, k, out, inbox, keep, send, recv, phase):
         self.k, self.out, self.inbox, self.keep = k, out, inbox, keep
@@ -233,8 +270,10 @@
             peer,
         )
 
+    phase_free = True
+
     def free(self, number):
-        if self.phase > 0:
+        if self.phase > 0 and self.phase_free:
             self.copy(number, self.phase - 1).wait_send()
 
     def across(self, value):
@@ -268,6 +307,155 @@
     def drain(self):
         for number in range(3):
             self.copy(number).wait_send()
+
+
+class ReduceColumns(Reduce):
+    def __init__(self, k, out, inbox, keep, send, recv, phase, chunks, sems):
+        super().__init__(k, out, inbox, keep, send, recv, phase)
+        self.chunks, self.part_send, self.part_recv = chunks, sems[0], sems[1]
+
+    def cols(self, chunk):
+        width = self.keep.shape[1] // self.chunks
+        return pl.ds(pl.multiple_of(chunk * width, width), width)
+
+    def part(self, number, n, chunk):
+        cols = self.cols(chunk)
+        return remote(
+            self.out.at[number, :, cols],
+            self.inbox.at[number, :, cols],
+            self.part_send.at[number, n],
+            self.part_recv.at[number, n],
+            self.k.y_peer if number == 2 else self.k.c_peer,
+        )
+
+    def step(self, n, chunk, block):
+        cols = self.cols(chunk)
+        if n == 0:
+            for number in range(3):
+                self.free(number)
+        self.out[0, :, cols] = block("across").astype(BF16)
+        self.part(0, n, chunk).start()
+        self.out[1, :, cols] = block("partner").astype(BF16)
+        self.part(1, n, chunk).start()
+        value = block("theirs")
+        self.part(0, n, chunk).wait_recv()
+        self.out[2, :, cols] = (value + self.inbox[0, :, cols].astype(F32)).astype(BF16)
+        self.part(2, n, chunk).start()
+        self.keep[:, cols] = block("mine")
+
+    def wait_columns(self, order):
+        for n, chunk in enumerate(order):
+            self.part(1, n, chunk).wait_recv()
+            self.part(2, n, chunk).wait_recv()
+
+    def drain_columns(self, order):
+        for n, chunk in enumerate(order):
+            for number in range(3):
+                self.part(number, n, chunk).wait_send()
+
+
+class DownWeights:
+    HALVES = 2
+
+    def __init__(self, k, full, start, size, sems):
+        self.k, self.full, self.start_at, self.half = k, full, start, size // self.HALVES
+        self.z_send, self.z_recv, self.x_send, self.x_recv = sems
+
+    def shard(self, step, x, half):
+        z = lax.rem(self.k.z - step + self.k.outer, self.k.outer)
+        return self.full.at[z, x, :, pl.ds(self.start_at + half * self.half, self.half)]
+
+    def first(self, step, half):
+        block = self.shard(0, self.k.x, half)
+        sems = (self.z_send.at[step, half], self.z_recv.at[step, half])
+        return remote(block, block, *sems, self.k.z_peer(step))
+
+    def arrived(self, step, half):
+        block = self.shard(step, self.k.x, half)
+        sems = (self.z_send.at[step, half], self.z_recv.at[step, half])
+        return remote(block, block, *sems, self.k.z_peer(step))
+
+    def second(self, step, half, x):
+        block = self.shard(step, x, half)
+        sems = (self.x_send.at[step, half], self.x_recv.at[step, half])
+        return remote(block, block, *sems, self.k.x_peer)
+
+    def start(self, step):
+        for half in range(self.HALVES):
+            self.first(step, half).start()
+
+    def forward(self, step):
+        for half in range(self.HALVES):
+            if step > 0:
+                self.arrived(step, half).wait_recv()
+            self.second(step, half, self.k.x).start()
+
+    def arrive(self, step):
+        for half in range(self.HALVES):
+            self.second(step, half, 1 - self.k.x).wait_recv()
+
+    def drain(self):
+        for step in range(self.k.outer):
+            for half in range(self.HALVES):
+                if step > 0:
+                    self.first(step, half).wait_send()
+                self.second(step, half, self.k.x).wait_send()
+
+
+class DownGradient:
+    def __init__(self, k, part, near, far, start, size, sems):
+        self.k, self.part, self.near, self.far = k, part, near, far
+        self.cols = pl.ds(start, size)
+        self.x_send, self.x_recv, self.z_send, self.z_recv = sems
+
+    def one(self, step):
+        k = self.k
+        z = lax.rem(k.z + step, k.outer)
+        return remote(
+            self.part.at[z, 1 - k.x, :, self.cols],
+            self.near.at[z, :, self.cols],
+            self.x_send.at[step],
+            self.x_recv.at[step],
+            k.x_peer,
+        )
+
+    def two(self, step):
+        k = self.k
+        return remote(
+            self.part.at[lax.rem(k.z + step, k.outer), k.x, :, self.cols],
+            self.far.at[step - 1, :, self.cols],
+            self.z_send.at[step],
+            self.z_recv.at[step],
+            k.z_peer(step),
+        )
+
+    def start(self, step):
+        self.one(step).start()
+
+    def forward(self, step):
+        k = self.k
+        z = lax.rem(k.z + step, k.outer)
+        self.one(step).wait_recv()
+        here = self.part[z, k.x, :, self.cols].astype(F32)
+        self.part[z, k.x, :, self.cols] = (
+            here + self.near[z, :, self.cols].astype(F32)
+        ).astype(BF16)
+        if step > 0:
+            self.two(step).start()
+
+    def finish(self, out):
+        k = self.k
+        total = self.part[k.z, k.x, :, self.cols].astype(F32)
+        for step in range(1, k.outer):
+            self.two(step).wait_recv()
+            total = total + self.far[step - 1, :, self.cols].astype(F32)
+        out[...] = total.T
+
+    def drain(self):
+        for step in range(self.k.outer):
+            self.one(step).wait_send()
+            if step > 0:
+                self.two(step).wait_send()
 
 
 def fold(values):
@@ -352,6 +540,10 @@
     v_send,
     v_recv,
     load_sem,
+    dw_sems,
+    dg_sems,
+    rc_sems,
+    sc_sems,
 ):
     k = Place(outer)
     rows, model = x_in.shape
@@ -386,7 +578,6 @@
     load(ub_in, VEC.at[pl.ds(8, 1), :])
     k.greet()
 
-    weights = Weights(k, W, w_send, w_recv, width, pieces)
 
     def keep(p, total):
         if p < 3:
@@ -399,6 +590,16 @@
             gd_ref[(p - down_piece) * width : (p - down_piece + 1) * width, :] = total.T
 
     grads = Gradients(k, G, near, far, keep, g_send, g_recv, width)
+    stepped = outer == 4 and (model // outer) % 128 == 0
+    simple = down_piece if stepped else pieces
+    weights = Weights(k, W, w_send, w_recv, width, simple)
+    if stepped:
+        down_w = DownWeights(k, W, down_piece * width, inner, dw_sems)
+        down_g = DownGradient(k, G, near, far, down_piece * width, inner, dg_sems)
+    w_order = (0, 1, 3, 2)
+    w_chunks = [lax.rem(k.z - step + outer, outer) for step in w_order]
+    g_order = (2, 1, 3, 0)
+    g_chunks = [lax.rem(k.z + step, outer) for step in g_order]
 
     def spread(blocks, phase):
         return Spread(k, blocks, s_send, s_recv, phase)
@@ -488,9 +689,14 @@
     r0.theirs(out_block(theirs, k.c))
     attend(mine)
     weights.forward(5)
+    if stepped:
+        down_w.start(1)
     r0.partner(out_block(mine, 1 - k.c))
     r0.mine(out_block(mine, k.c))
     weights.forward(6)
+    if stepped:
+        down_w.start(3)
+        down_w.start(2)
     r0.wait()
 
     def first_norm(r):
@@ -508,7 +714,10 @@
     s1 = spread(H, 1)
     s1.start()
     weights.forward(7)
-    weights.forward(8)
+    if stepped:
+        down_w.forward(0)
+    else:
+        weights.forward(8)
     s1.own()
     for p in range(up_piece, down_piece):
         weights.arrive(p)
@@ -531,21 +740,57 @@
     def down_block(seq, core):
         return dot(ACT[seq, part_rows(core), :], matrix(down_piece * width, inner), NT)
 
-    up(mine)
-    weights.forward(9)
-    s1.pass_on()
-    s1.other()
-    up(theirs)
-    weights.forward(10)
-    weights.forward(11)
-    for p in range(down_piece, pieces):
-        weights.arrive(p)
-    r1 = reduce(1)
-    r1.across(down_block(theirs, 1 - k.c))
-    r1.theirs(down_block(theirs, k.c))
-    r1.partner(down_block(mine, 1 - k.c))
-    r1.mine(down_block(mine, k.c))
-    r1.wait()
+    if stepped:
+        up(mine)
+        down_w.forward(1)
+        down_w.forward(3)
+        s1.pass_on()
+        s1.other()
+        up(theirs)
+        r1 = ReduceColumns(k, OUTBOX, INBOX, OWN, r_send, r_recv, 1, outer, rc_sems)
+        places = {
+            "across": (theirs, 1 - k.c),
+            "theirs": (theirs, k.c),
+            "partner": (mine, 1 - k.c),
+            "mine": (mine, k.c),
+        }
+
+        def down_chunk(n):
+            shard = W[w_chunks[n], :, :, pl.ds(down_piece * width, inner)]
+            shard = shard.reshape(model // outer, inner)
+
+            def block(name):
+                seq, core = places[name]
+                return dot(ACT[seq, part_rows(core), :], shard, NT)
+
+            r1.step(n, w_chunks[n], block)
+
+        down_w.arrive(0)
+        down_chunk(0)
+        down_w.forward(2)
+        down_w.arrive(1)
+        down_chunk(1)
+        down_w.arrive(3)
+        down_chunk(2)
+        down_w.arrive(2)
+        down_chunk(3)
+        r1.wait_columns(w_chunks)
+    else:
+        up(mine)
+        weights.forward(9)
+        s1.pass_on()
+        s1.other()
+        up(theirs)
+        weights.forward(10)
+        weights.forward(11)
+        for p in range(down_piece, pieces):
+            weights.arrive(p)
+        r1 = reduce(1)
+        r1.across(down_block(theirs, 1 - k.c))
+        r1.theirs(down_block(theirs, k.c))
+        r1.partner(down_block(mine, 1 - k.c))
+        r1.mine(down_block(mine, k.c))
+        r1.wait()
 
     def norm_back(d, gain, normed, scaling):
         e = d * gain
@@ -568,8 +813,12 @@
         SUMS[3] += fold(diff * diff)
 
     norm_loop(second_norm)
-    s2 = spread(MX, 2)
-    s2.start()
+    if stepped:
+        s2 = SpreadColumns(k, MX, s_send, s_recv, 2, outer, sc_sems)
+        s2.start_columns(g_chunks)
+    else:
+        s2 = spread(MX, 2)
+        s2.start()
     s2.own()
 
     def back_up(seq):
@@ -606,23 +855,53 @@
         lax.fori_loop(begin, end, piece, 0)
 
     r2 = reduce(2)
+    if stepped:
+        r1.drain_columns(w_chunks)
+        r2.phase_free = False
     back_up(mine)
     r2.partner(hidden_block(mine, 1 - k.c))
     r2.mine(hidden_block(mine, k.c))
-    s2.pass_on()
-    s2.other()
-    weight_grad(MX, ACT, down_piece, 0, 2)
-    back_up(theirs)
-    grads.start(down_piece + 1)
-    r2.across(hidden_block(theirs, 1 - k.c))
-    r2.theirs(hidden_block(theirs, k.c))
-    weight_grad(MX, ACT, down_piece, 2, steps)
-    grads.forward(8)
-    grads.start(down_piece + steps - 1)
-    weight_grad(H, GU, up_piece, 0, steps)
-    grads.start(up_piece + steps - 1)
-    grads.forward(9)
-    grads.forward(10)
+    if stepped:
+
+        def down_grad_chunk(n):
+            tokens, size = 4 * rows, model // outer
+            cols = pl.ds(pl.multiple_of(g_chunks[n] * size, size), size)
+            grad = dot(
+                MX[:, :, cols].reshape(tokens, size), ACT[...].reshape(tokens, inner), TN
+            )
+            G[g_chunks[n], :, :, pl.ds(down_piece * width, inner)] = grad.astype(BF16).reshape(
+                2, size // 2, inner
+            )
+
+        for n in range(outer):
+            s2.pass_part(n, g_chunks[n])
+            s2.other_part(n, g_chunks[n])
+            down_grad_chunk(n)
+            down_g.start(g_order[n])
+        back_up(theirs)
+        r2.across(hidden_block(theirs, 1 - k.c))
+        down_g.forward(g_order[0])
+        r2.theirs(hidden_block(theirs, k.c))
+        down_g.forward(g_order[1])
+        weight_grad(H, GU, up_piece, 0, steps)
+        grads.start(up_piece + steps - 1)
+        down_g.forward(g_order[2])
+        down_g.forward(g_order[3])
+    else:
+        s2.pass_on()
+        s2.other()
+        weight_grad(MX, ACT, down_piece, 0, 2)
+        back_up(theirs)
+        grads.start(down_piece + 1)
+        r2.across(hidden_block(theirs, 1 - k.c))
+        r2.theirs(hidden_block(theirs, k.c))
+        weight_grad(MX, ACT, down_piece, 2, steps)
+        grads.forward(8)
+        grads.start(down_piece + steps - 1)
+        weight_grad(H, GU, up_piece, 0, steps)
+        grads.start(up_piece + steps - 1)
+        grads.forward(9)
+        grads.forward(10)
     r2.wait()
 
     def first_back(r):
@@ -665,15 +944,20 @@
     def input_block(seq, core):
         return dot(DQKV[seq, part_rows(core), :], matrix(0, 3 * width), NT)
 
+    if stepped:
+        grads.forward(4)
     attend_back(mine)
-    grads.forward(11)
+    grads.forward(5 if stepped else 11)
     s3.pass_on()
-    grads.forward(4)
+    grads.forward(6 if stepped else 4)
     s3.other()
     weight_grad(GF, C, 3, 0, 1)
-    grads.forward(5)
+    if not stepped:
+        grads.forward(5)
     attend_back(theirs)
     grads.start(3)
+    if stepped:
+        grads.forward(7)
 
     here = pl.ds(pl.multiple_of(k.t * width, width), width)
     for row, n in ((0, 0), (1, 2)):
@@ -703,18 +987,21 @@
     hops[1].start()
     weight_grad(X, DQKV, 0, 2, 3)
     grads.start(1)
-    grads.forward(6)
+    if not stepped:
+        grads.forward(6)
     r3 = reduce(3)
     r3.across(input_block(theirs, 1 - k.c))
     r3.theirs(input_block(theirs, k.c))
     hop_in(1)
     hops[2].start()
     grads.start(2)
-    grads.forward(7)
+    if not stepped:
+        grads.forward(7)
     r3.partner(input_block(mine, 1 - k.c))
     r3.mine(input_block(mine, k.c))
-    for p in (8, 9, 10):
-        grads.finish(p)
+    if not stepped:
+        for p in (8, 9, 10):
+            grads.finish(p)
     grads.forward(3)
     grads.forward(0)
     grads.forward(1)
@@ -733,7 +1020,11 @@
         gin_ref[r, :] = GS[r, :] + r3.total(r)
 
     norm_loop(last)
-    for p in (11, 4, 5, 6, 7, 3, 0, 1):
+    if stepped:
+        down_g.finish(gd_ref)
+    else:
+        grads.finish(11)
+    for p in (4, 5, 6, 7, 3, 0, 1):
         grads.finish(p)
     vz_all = VZ.at[pl.ds(0, outer - 1)]
     every = remote(vz_all, vz_all, v_send.at[3], v_recv.at[3], k.x_peer)
@@ -745,9 +1036,13 @@
     gvec_ref[...] = lax.fori_loop(1, outer, add, VZ[0])
     grads.finish(2)
 
-    weights.drain(pieces)
-    grads.drain(pieces)
-    for s in (s0, s1, s2, s3):
+    weights.drain(simple)
+    grads.drain(simple)
+    if stepped:
+        down_w.drain()
+        down_g.drain()
+        s2.drain_columns(g_chunks)
+    for s in (s0, s1, s3) if stepped else (s0, s1, s2, s3):
         s.drain()
     r3.drain()
     for hop in hops:
@@ -830,6 +1125,10 @@
             dma((4,)),
             dma((4,)),
             dma((len(arrays),)),
+            (dma((outer, 2)),) * 4,
+            (dma((outer,)),) * 4,
+            (dma((3, outer)),) * 2,
+            (dma((outer,)),) * 4,
         ],
         compiler_params=pltpu.CompilerParams(
             collective_id=0, has_side_effects=True, vmem_limit_bytes=67043328

time: 222 us -> 204 us (0.919)
  Pallas kernels: 218 us -> 200 us
    pallas_call x1, Pallas kernels: 214 us -> 197 us  [layer(): pl.pallas_call(functools.partial(body, outer), out_shape=outs, in_specs=[...]
where the time goes in v3:
time: 204 us
  Pallas kernels  200 us (98%)
  between operations  2.46 us (1%)
    pallas_call x1, Pallas kernels, layer(): pl.pallas_call(functools.partial(body, outer), out_shape=outs, in_specs=[...  197 us

profile of v3, /device:TPU:0, one launch (start us, length us, event | category | flops | bytes accessed | tf_op | source)
XLA Modules:
  0.0 204.1 jit_solution(16754117780152593943)
XLA Ops:
  0.7 196.6 %layer.1 = (bf16[256,1024]{1,0:T(8,128)(2,1)}, f32[256,1024]{1,0:T(8,128)}, f32[128,256]{1,0:T(8,128)}, f32[128,256]{1,0:T(8,128)}, f32[128,256]{1,0:T(8,128)}, ...) custom-call(bf16[256,1024]{1,0:T(8,128)(2,1)} %x_in.1, ...), custom_call_target="tpu_custom_call" | custom-call | tf_op jit(solution)/shard_map/layer/pallas_call | solution.py:1077
  197.3 3.7 %write.1 = (bf16[256,1024]{1,0:T(8,128)(2,1)}, f32[256,1024]{1,0:T(8,128)}, f32[128,256]{1,0:T(8,128)}, f32[128,256]{1,0:T(8,128)}, f32[128,256]{1,0:T(8,128)}, ...) custom-call(bf16[256,1024]{1,0:T(8,128)(2,1)} %get-tuple-element.45., ...), custom_call_target="tpu_custom_call" | custom-call | tf_op jit(solution)/shard_map/write/pallas_call | solution.py:1163
  201.0 0.0 copy-start
  201.0 0.7 copy-done
  201.7 0.6 reduce_sum.9
Async XLA Ops:
  201.0 0.7 copy-start

commit v4 on v3

--- a/solution.py
+++ b/solution.py
@@ -178,6 +178,152 @@
         lax.fori_loop(0, pieces, piece, 0)
 
 
+class Line:
+    def __init__(self, k):
+        self.k = k
+        self.two = lax.rem(k.z + 2, 4)
+        self.next = k.z + 1 - 2 * lax.rem(k.z, 2)
+        self.third = 3 - k.z
+        self.middle = (k.z == 1) | (k.z == 2)
+        self.end = (k.z == 0) | (k.z == 3)
+
+    def peer(self, z):
+        return (z * 2 + self.k.x, self.k.t)
+
+
+class LineWeights(Weights):
+    def __init__(self, line, *rest):
+        super().__init__(line.k, *rest)
+        self.line = line
+
+    def send_to(self, z, source, send, recv, p):
+        block = self.full.at[source, self.k.x, :, columns(p, self.width)]
+        return remote(
+            block, block, self.send.at[send, p], self.recv.at[recv, p], self.line.peer(z)
+        )
+
+    def some(self, count, send, recv, p):
+        block = self.full.at[pl.ds(0, count), 0, :, columns(p, self.width)]
+        return remote(block, block, self.send.at[send, p], self.recv.at[recv, p], self.k.x_peer)
+
+    def start(self, p):
+        line = self.line
+        self.send_to(line.two, self.k.z, 0, 0, p).start()
+        self.send_to(line.next, self.k.z, 0, 0, p).start()
+
+        @pl.when(line.middle)
+        def _():
+            self.send_to(line.third, self.k.z, 2, 2, p).start()
+
+    def relay(self, p):
+        line = self.line
+        self.some(2, 0, 0, p).wait_recv()
+
+        @pl.when(line.middle)
+        def _():
+            self.send_to(line.next, line.two, 3, 2, p).start()
+
+        if p + WINDOW < self.pieces:
+            self.start(p + WINDOW)
+
+    def forward(self, p):
+        self.some(1, 2, 2, p).wait_recv()
+        self.second(p).start()
+
+    def drain(self, pieces):
+        def piece(p, carry):
+            self.some(2, 0, 0, p).wait_send()
+            self.second(p).wait_send()
+
+            @pl.when(self.line.middle)
+            def _():
+                self.some(1, 2, 2, p).wait_send()
+                self.some(1, 3, 2, p).wait_send()
+
+            return carry
+
+        lax.fori_loop(0, pieces, piece, 0)
+
+
+class LineGradients(Gradients):
+    def __init__(self, line, hop, *rest):
+        super().__init__(line.k, *rest)
+        self.line, self.hop = line, hop
+
+    def to(self, z, dst, send, recv, p):
+        cols = columns(p, self.width)
+        return remote(
+            self.part.at[z, self.k.x, :, cols],
+            dst.at[:, cols],
+            self.send.at[send, p],
+            self.recv.at[recv, p],
+            self.line.peer(z),
+        )
+
+    def to_hop(self, p):
+        cols = columns(p, self.width)
+        return remote(
+            self.part.at[self.line.third, self.k.x, :, cols],
+            self.hop.at[:, cols],
+            self.send.at[2, p],
+            self.recv.at[3, p],
+            self.line.peer(self.line.next),
+        )
+
+    def forward(self, p):
+        k, line, cols = self.k, self.line, columns(p, self.width)
+        self.one(p).wait_recv()
+        here = self.part[:, k.x, :, cols].astype(F32)
+        self.part[:, k.x, :, cols] = (here + self.near[:, :, cols].astype(F32)).astype(BF16)
+
+        @pl.when(line.end)
+        def _():
+            self.to_hop(p).start()
+            self.to(line.two, self.far.at[0], 3, 1, p).start()
+
+        @pl.when(line.middle)
+        def _():
+            self.to(line.third, self.far.at[2], 2, 2, p).start()
+
+        self.to(line.next, self.far.at[1], 1, 1, p).start()
+
+    def relay(self, p):
+        line, cols = self.line, columns(p, self.width)
+
+        @pl.when(line.middle)
+        def _():
+            self.to_hop(p).wait_recv()
+            here = self.part[line.two, self.k.x, :, cols].astype(F32)
+            here = here + self.hop[:, cols].astype(F32)
+            self.part[line.two, self.k.x, :, cols] = here.astype(BF16)
+            self.to(line.two, self.far.at[0], 3, 1, p).start()
+
+    def finish(self, p):
+        k, line, cols = self.k, self.line, columns(p, self.width)
+        both = self.far.at[pl.ds(0, 2), :, cols]
+        remote(both, both, self.send.at[1, p], self.recv.at[1, p], k.x_peer).wait_recv()
+
+        @pl.when(line.middle)
+        def _():
+            self.to(line.third, self.far.at[2], 2, 2, p).wait_recv()
+
+        total = self.part[k.z, k.x, :, cols].astype(F32)
+        for n in range(3):
+            total = total + self.far[n, :, cols].astype(F32)
+        self.out(p, total)
+
+    def drain(self, pieces):
+        line = self.line
+
+        def piece(p, carry):
+            self.one(p).wait_send()
+            for z, sem in ((line.next, 1), (line.third, 2), (line.two, 3)):
+                self.to(z, self.far.at[0], sem, 1, p).wait_send()
+            return carry
+
+        lax.fori_loop(0, pieces, piece, 0)
+
+
 class Spread:
     def __init__(self, k, blocks, send, recv, phase):
         self.k, self.blocks, self.send, self.recv, self.phase = k, blocks, send, recv, phase
@@ -357,105 +503,147 @@
 class DownWeights:
     HALVES = 2
 
-    def __init__(self, k, full, start, size, sems):
-        self.k, self.full, self.start_at, self.half = k, full, start, size // self.HALVES
+    def __init__(self, line, full, start, size, sems):
+        self.line, self.k = line, line.k
+        self.full, self.start_at, self.half = full, start, size // self.HALVES
         self.z_send, self.z_recv, self.x_send, self.x_recv = sems
-
-    def shard(self, step, x, half):
-        z = lax.rem(self.k.z - step + self.k.outer, self.k.outer)
+        self.sources = (self.k.z, line.two, line.next, line.third)
+
+    def shard(self, z, x, half):
         return self.full.at[z, x, :, pl.ds(self.start_at + half * self.half, self.half)]
 
-    def first(self, step, half):
-        block = self.shard(0, self.k.x, half)
-        sems = (self.z_send.at[step, half], self.z_recv.at[step, half])
-        return remote(block, block, *sems, self.k.z_peer(step))
-
-    def arrived(self, step, half):
-        block = self.shard(step, self.k.x, half)
-        sems = (self.z_send.at[step, half], self.z_recv.at[step, half])
-        return remote(block, block, *sems, self.k.z_peer(step))
-
-    def second(self, step, half, x):
-        block = self.shard(step, x, half)
+    def along(self, z, source, send, recv, half):
+        block = self.shard(source, self.k.x, half)
+        sems = (self.z_send.at[send, half], self.z_recv.at[recv, half])
+        return remote(block, block, *sems, self.line.peer(z))
+
+    def across(self, step, half, x):
+        block = self.shard(self.sources[step], x, half)
         sems = (self.x_send.at[step, half], self.x_recv.at[step, half])
         return remote(block, block, *sems, self.k.x_peer)
 
     def start(self, step):
+        z = self.sources[step]
         for half in range(self.HALVES):
-            self.first(step, half).start()
+            if step < 3:
+                self.along(z, self.k.z, step, step, half).start()
+            else:
+
+                @pl.when(self.line.middle)
+                def _():
+                    self.along(z, self.k.z, 3, 3, half).start()
 
     def forward(self, step):
         for half in range(self.HALVES):
             if step > 0:
-                self.arrived(step, half).wait_recv()
-            self.second(step, half, self.k.x).start()
+                self.along(self.line.next, self.k.z, step, step, half).wait_recv()
+            if step == 1:
+
+                @pl.when(self.line.middle)
+                def _():
+                    self.along(self.line.next, self.line.two, 0, 3, half).start()
+
+            self.across(step, half, self.k.x).start()
 
     def arrive(self, step):
         for half in range(self.HALVES):
-            self.second(step, half, 1 - self.k.x).wait_recv()
+            self.across(step, half, 1 - self.k.x).wait_recv()
 
     def drain(self):
-        for step in range(self.k.outer):
-            for half in range(self.HALVES):
-                if step > 0:
-                    self.first(step, half).wait_send()
-                self.second(step, half, self.k.x).wait_send()
+        for half in range(self.HALVES):
+            for step in range(4):
+                self.across(step, half, self.k.x).wait_send()
+            for step in (1, 2):
+                self.along(self.line.next, self.k.z, step, step, half).wait_send()
+
+            @pl.when(self.line.middle)
+            def _():
+                for sem in (3, 0):
+                    self.along(self.line.next, self.k.z, sem, 3, half).wait_send()
 
 
 class DownGradient:
-    def __init__(self, k, part, near, far, start, size, sems):
-        self.k, self.part, self.near, self.far = k, part, near, far
+    def __init__(self, line, part, near, far, hop, start, size, sems):
+        self.line, self.k = line, line.k
+        self.part, self.near, self.far, self.hop = part, near, far, hop
         self.cols = pl.ds(start, size)
         self.x_send, self.x_recv, self.z_send, self.z_recv = sems
+        self.targets = (line.third, line.next, line.two, self.k.z)
 
     def one(self, step):
-        k = self.k
-        z = lax.rem(k.z + step, k.outer)
+        z = self.targets[step]
         return remote(
-            self.part.at[z, 1 - k.x, :, self.cols],
+            self.part.at[z, 1 - self.k.x, :, self.cols],
             self.near.at[z, :, self.cols],
             self.x_send.at[step],
             self.x_recv.at[step],
-            k.x_peer,
+            self.k.x_peer,
         )
 
-    def two(self, step):
-        k = self.k
+    def along(self, step, dst, recv, peer):
         return remote(
-            self.part.at[lax.rem(k.z + step, k.outer), k.x, :, self.cols],
-            self.far.at[step - 1, :, self.cols],
+            self.part.at[self.targets[step], self.k.x, :, self.cols],
+            dst.at[:, self.cols],
             self.z_send.at[step],
-            self.z_recv.at[step],
-            k.z_peer(step),
+            self.z_recv.at[recv],
+            self.line.peer(peer),
         )
 
     def start(self, step):
         self.one(step).start()
 
     def forward(self, step):
-        k = self.k
-        z = lax.rem(k.z + step, k.outer)
+        k, line, z = self.k, self.line, self.targets[step]
         self.one(step).wait_recv()
         here = self.part[z, k.x, :, self.cols].astype(F32)
-        self.part[z, k.x, :, self.cols] = (
-            here + self.near[z, :, self.cols].astype(F32)
-        ).astype(BF16)
-        if step > 0:
-            self.two(step).start()
+        here = here + self.near[z, :, self.cols].astype(F32)
+        if step != 2:
+            self.part[z, k.x, :, self.cols] = here.astype(BF16)
+        if step == 0:
+
+            @pl.when(line.end)
+            def _():
+                self.along(0, self.hop, 3, line.next).start()
+
+            @pl.when(line.middle)
+            def _():
+                self.along(0, self.far.at[2], 0, line.third).start()
+
+        if step == 1:
+            self.along(1, self.far.at[1], 1, line.next).start()
+        if step == 2:
+
+            @pl.when(line.end)
+            def _():
+                self.part[z, k.x, :, self.cols] = here.astype(BF16)
+
+            @pl.when(line.middle)
+            def _():
+                self.along(0, self.hop, 3, line.next).wait_recv()
+                both = here + self.hop[:, self.cols].astype(F32)
+                self.part[z, k.x, :, self.cols] = both.astype(BF16)
+
+            self.along(2, self.far.at[0], 2, line.two).start()
 
     def finish(self, out):
         k = self.k
+
+        @pl.when(self.line.middle)
+        def _():
+            self.along(0, self.far.at[2], 0, k.z).wait_recv()
+
         total = self.part[k.z, k.x, :, self.cols].astype(F32)
-        for step in range(1, k.outer):
-            self.two(step).wait_recv()
-            total = total + self.far[step - 1, :, self.cols].astype(F32)
+        for n in range(3):
+            if n < 2:
+                self.along(0, self.far.at[n], 2 - n, k.z).wait_recv()
+            total = total + self.far[n, :, self.cols].astype(F32)
         out[...] = total.T
 
     def drain(self):
-        for step in range(self.k.outer):
+        for step in range(4):
             self.one(step).wait_send()
-            if step > 0:
-                self.two(step).wait_send()
+            if step < 3:
+                self.along(step, self.far.at[0], 0, self.k.z).wait_send()
 
 
 def fold(values):
@@ -540,6 +728,7 @@
     v_send,
     v_recv,
     load_sem,
+    HOP,
     dw_sems,
     dg_sems,
     rc_sems,
@@ -589,17 +778,26 @@
         else:
             gd_ref[(p - down_piece) * width : (p - down_piece + 1) * width, :] = total.T
 
-    grads = Gradients(k, G, near, far, keep, g_send, g_recv, width)
     stepped = outer == 4 and (model // outer) % 128 == 0
     simple = down_piece if stepped else pieces
-    weights = Weights(k, W, w_send, w_recv, width, simple)
     if stepped:
-        down_w = DownWeights(k, W, down_piece * width, inner, dw_sems)
-        down_g = DownGradient(k, G, near, far, down_piece * width, inner, dg_sems)
-    w_order = (0, 1, 3, 2)
-    w_chunks = [lax.rem(k.z - step + outer, outer) for step in w_order]
-    g_order = (2, 1, 3, 0)
-    g_chunks = [lax.rem(k.z + step, outer) for step in g_order]
+        line = Line(k)
+        weights = LineWeights(line, W, w_send, w_recv, width, simple)
+        grads = LineGradients(line, HOP, G, near, far, keep, g_send, g_recv, width)
+        down_w = DownWeights(line, W, down_piece * width, inner, dw_sems)
+        down_g = DownGradient(line, G, near, far, HOP, down_piece * width, inner, dg_sems)
+        w_chunks, g_chunks = down_w.sources, down_g.targets
+    else:
+        weights = Weights(k, W, w_send, w_recv, width, simple)
+        grads = Gradients(k, G, near, far, keep, g_send, g_recv, width)
+
+    def relay(p):
+        if stepped and p < simple:
+            weights.relay(p)
+
+    def relay_back(p):
+        if stepped:
+            grads.relay(p)
 
     def spread(blocks, phase):
         return Spread(k, blocks, s_send, s_recv, phase)
@@ -628,6 +826,8 @@
 
     SUMS[...] = jnp.zeros_like(SUMS)
     VA[0] = jnp.zeros_like(VA[0])
+    if stepped:
+        far[2] = jnp.zeros_like(far[2])
     for copy in loads:
         copy.wait()
     own[:, columns(3, width)] = OT[...].T
@@ -671,32 +871,40 @@
     def out_block(seq, core):
         return dot(C[seq, part_rows(core), :], matrix(3 * width, width), NT)
 
+    relay(0)
     weights.forward(0)
+    relay(1)
+    relay(2)
     weights.forward(1)
     s0.pass_on()
     s0.own()
     s0.other()
     project(0, Q)
+    relay(3)
     weights.forward(2)
     project(1, K)
+    relay(4)
     weights.forward(3)
     project(2, V)
     r0 = reduce(0)
     attend(theirs)
+    relay(5)
     weights.forward(4)
     weights.arrive(3)
     r0.across(out_block(theirs, 1 - k.c))
     r0.theirs(out_block(theirs, k.c))
+    relay(6)
     attend(mine)
     weights.forward(5)
+    relay(7)
     if stepped:
         down_w.start(1)
     r0.partner(out_block(mine, 1 - k.c))
     r0.mine(out_block(mine, k.c))
     weights.forward(6)
     if stepped:
+        down_w.start(2)
         down_w.start(3)
-        down_w.start(2)
     r0.wait()
 
     def first_norm(r):
@@ -743,7 +951,7 @@
     if stepped:
         up(mine)
         down_w.forward(1)
-        down_w.forward(3)
+        down_w.forward(2)
         s1.pass_on()
         s1.other()
         up(theirs)
@@ -767,13 +975,10 @@
 
         down_w.arrive(0)
         down_chunk(0)
-        down_w.forward(2)
-        down_w.arrive(1)
-        down_chunk(1)
-        down_w.arrive(3)
-        down_chunk(2)
-        down_w.arrive(2)
-        down_chunk(3)
+        down_w.forward(3)
+        for n in range(1, outer):
+            down_w.arrive(n)
+            down_chunk(n)
         r1.wait_columns(w_chunks)
     else:
         up(mine)
@@ -877,16 +1082,16 @@
             s2.pass_part(n, g_chunks[n])
             s2.other_part(n, g_chunks[n])
             down_grad_chunk(n)
-            down_g.start(g_order[n])
+            down_g.start(n)
         back_up(theirs)
         r2.across(hidden_block(theirs, 1 - k.c))
-        down_g.forward(g_order[0])
+        down_g.forward(0)
         r2.theirs(hidden_block(theirs, k.c))
-        down_g.forward(g_order[1])
+        down_g.forward(1)
         weight_grad(H, GU, up_piece, 0, steps)
         grads.start(up_piece + steps - 1)
-        down_g.forward(g_order[2])
-        down_g.forward(g_order[3])
+        down_g.forward(2)
+        down_g.forward(3)
     else:
         s2.pass_on()
         s2.other()
@@ -947,8 +1152,10 @@
     if stepped:
         grads.forward(4)
     attend_back(mine)
+    relay_back(4)
     grads.forward(5 if stepped else 11)
     s3.pass_on()
+    relay_back(5)
     grads.forward(6 if stepped else 4)
     s3.other()
     weight_grad(GF, C, 3, 0, 1)
@@ -956,6 +1163,7 @@
         grads.forward(5)
     attend_back(theirs)
     grads.start(3)
+    relay_back(6)
     if stepped:
         grads.forward(7)
 
@@ -1002,9 +1210,13 @@
     if not stepped:
         for p in (8, 9, 10):
             grads.finish(p)
+    relay_back(7)
     grads.forward(3)
+    relay_back(3)
     grads.forward(0)
+    relay_back(0)
     grads.forward(1)
+    relay_back(1)
     hop_in(2)
     VZ[k.z] = VA[3]
 
@@ -1014,6 +1226,7 @@
 
     lax.fori_loop(1, outer, send_last, 0)
     grads.forward(2)
+    relay_back(2)
     r3.wait()
 
     def last(r):
@@ -1114,10 +1327,10 @@
             pltpu.VMEM((width, shard_rows), BF16),
             pltpu.VMEM((inner, shard_rows), BF16),
             pltpu.VMEM((9, 4 * inner), F32),
-            dma((2, pieces)),
-            dma((2, pieces)),
-            dma((2, pieces)),
-            dma((2, pieces)),
+            dma((4, pieces)),
+            dma((4, pieces)),
+            dma((4, pieces)),
+            dma((4, pieces)),
             dma((4, 3)),
             dma((4, 3)),
             dma((4, 3)),
@@ -1125,6 +1338,7 @@
             dma((4,)),
             dma((4,)),
             dma((len(arrays),)),
+            pltpu.VMEM((shard_rows, columns_all), BF16),
             (dma((outer, 2)),) * 4,
             (dma((outer,)),) * 4,
             (dma((3, outer)),) * 2,

time: 204 us -> 198 us (0.971)
  Pallas kernels: 200 us -> 194 us
    pallas_call x1, Pallas kernels: 197 us -> 190 us  [layer(): pl.pallas_call(functools.partial(body, outer), out_shape=outs, in_specs=[...]
where the time goes in v4:
time: 198 us; the launch traced here: 197 us
  Pallas kernels  194 us (98%)
  between operations  2.46 us (1%)
    pallas_call x1, Pallas kernels, layer(): pl.pallas_call(functools.partial(body, outer), out_shape=outs, in_specs=[...  190 us

profile of v4, /device:TPU:0, one launch (start us, length us, event | category | flops | bytes accessed | tf_op | source)
XLA Modules:
  0.0 197.4 jit_solution(14246660291313002308)
XLA Ops:
  0.7 190.0 %layer.1 = (bf16[256,1024]{1,0:T(8,128)(2,1)}, f32[256,1024]{1,0:T(8,128)}, f32[128,256]{1,0:T(8,128)}, f32[128,256]{1,0:T(8,128)}, f32[128,256]{1,0:T(8,128)}, ...) custom-call(bf16[256,1024]{1,0:T(8,128)(2,1)} %x_in.1, ...), custom_call_target="tpu_custom_call" | custom-call | tf_op jit(solution)/shard_map/layer/pallas_call | solution.py:1290
  190.6 3.7 %write.1 = (bf16[256,1024]{1,0:T(8,128)(2,1)}, f32[256,1024]{1,0:T(8,128)}, f32[128,256]{1,0:T(8,128)}, f32[128,256]{1,0:T(8,128)}, f32[128,256]{1,0:T(8,128)}, ...) custom-call(bf16[256,1024]{1,0:T(8,128)(2,1)} %get-tuple-element.45., ...), custom_call_target="tpu_custom_call" | custom-call | tf_op jit(solution)/shard_map/write/pallas_call | solution.py:1377
  194.3 0.0 copy-start
  194.4 0.7 copy-done
  195.0 0.6 reduce_sum.9
Async XLA Ops:
  194.3 0.7 copy-start

commit v5 on v4

--- a/solution.py
+++ b/solution.py
@@ -19,6 +19,8 @@
 TN = ((0,), (0,))
 CHUNK = 32
 WINDOW = 3
+CROSSED = (3, 7)
+CROSSED_BACK = (2, 7)
 ROOT_TWO = math.sqrt(2.0)
 ROOT_TWO_PI = math.sqrt(2.0 * math.pi)
 VECTORS = 16
@@ -196,18 +198,31 @@
         super().__init__(line.k, *rest)
         self.line = line
 
+    def shards(self, z, p):
+        return self.full.at[z, slice(None) if p in CROSSED else self.k.x, :, columns(p, self.width)]
+
     def send_to(self, z, source, send, recv, p):
-        block = self.full.at[source, self.k.x, :, columns(p, self.width)]
+        block = self.shards(source, p)
         return remote(
             block, block, self.send.at[send, p], self.recv.at[recv, p], self.line.peer(z)
         )
 
     def some(self, count, send, recv, p):
-        block = self.full.at[pl.ds(0, count), 0, :, columns(p, self.width)]
+        block = self.shards(pl.ds(0, count), p)
         return remote(block, block, self.send.at[send, p], self.recv.at[recv, p], self.k.x_peer)
+
+    def crossing(self, p):
+        block = self.full.at[self.k.z, self.k.x, :, columns(p, self.width)]
+        return remote(block, block, self.send.at[1, p], self.recv.at[1, p], self.k.x_peer)
+
+    def cross(self):
+        for p in CROSSED:
+            self.crossing(p).start()
 
     def start(self, p):
         line = self.line
+        if p in CROSSED:
+            self.crossing(p).wait_recv()
         self.send_to(line.two, self.k.z, 0, 0, p).start()
         self.send_to(line.next, self.k.z, 0, 0, p).start()
 
@@ -227,22 +242,111 @@
             self.start(p + WINDOW)
 
     def forward(self, p):
-        self.some(1, 2, 2, p).wait_recv()
-        self.second(p).start()
+        if p not in CROSSED:
+            self.some(1, 2, 2, p).wait_recv()
+            self.second(p).start()
+
+    def arrive(self, p):
+        if p in CROSSED:
+            self.some(1, 2, 2, p).wait_recv()
+        else:
+            self.second(p).wait_recv()
 
     def drain(self, pieces):
-        def piece(p, carry):
+        for p in range(pieces):
             self.some(2, 0, 0, p).wait_send()
-            self.second(p).wait_send()
-
-            @pl.when(self.line.middle)
-            def _():
+            (self.crossing(p) if p in CROSSED else self.second(p)).wait_send()
+
+        @pl.when(self.line.middle)
+        def _():
+            for p in range(pieces):
                 self.some(1, 2, 2, p).wait_send()
                 self.some(1, 3, 2, p).wait_send()
 
-            return carry
-
-        lax.fori_loop(0, pieces, piece, 0)
+
+class CrossedGradient:
+    def __init__(self, line, part, far, hop, last, out, send, recv, width, p, place):
+        self.line, self.k, self.part, self.out, self.p = line, line.k, part, out, p
+        self.far, self.hop, self.last = far.at[place], hop.at[place], last.at[place]
+        self.cols = columns(p, width)
+        self.send, self.recv = send, recv
+
+    def along(self, z, dst, send, recv, peer):
+        return remote(
+            self.part.at[z, :, :, self.cols],
+            dst,
+            self.send.at[send, self.p],
+            self.recv.at[recv, self.p],
+            self.line.peer(peer),
+        )
+
+    def to(self, z, slot, send, recv):
+        return self.along(z, self.far.at[slot], send, recv, z)
+
+    def to_hop(self):
+        return self.along(self.line.third, self.hop, 2, 3, self.line.next)
+
+    def over(self):
+        return remote(
+            self.part.at[self.k.z, 1 - self.k.x, :, self.cols],
+            self.last,
+            self.send.at[0, self.p],
+            self.recv.at[0, self.p],
+            self.k.x_peer,
+        )
+
+    def start(self):
+        line = self.line
+
+        @pl.when(line.end)
+        def _():
+            self.to_hop().start()
+            self.to(line.two, 0, 3, 1).start()
+
+        @pl.when(line.middle)
+        def _():
+            self.to(line.third, 2, 2, 2).start()
+
+        self.to(line.next, 1, 1, 1).start()
+
+    def relay(self):
+        line = self.line
+
+        @pl.when(line.middle)
+        def _():
+            self.to_hop().wait_recv()
+            here = self.part[line.two, :, :, self.cols].astype(F32) + self.hop[...].astype(F32)
+            self.part[line.two, :, :, self.cols] = here.astype(BF16)
+            self.to(line.two, 0, 3, 1).start()
+
+    def total(self, x):
+        total = self.part[self.k.z, x, :, self.cols].astype(F32)
+        for n in range(3):
+            total = total + self.far[n, x].astype(F32)
+        return total
+
+    def forward(self):
+        line = self.line
+        both = self.far.at[pl.ds(0, 2)]
+        remote(both, both, self.send.at[1, self.p], self.recv.at[1, self.p], self.k.x_peer).wait_recv()
+
+        @pl.when(line.middle)
+        def _():
+            self.to(line.third, 2, 2, 2).wait_recv()
+
+        x = 1 - self.k.x
+        self.part[self.k.z, x, :, self.cols] = self.total(x).astype(BF16)
+        self.over().start()
+
+    def finish(self):
+        self.over().wait_recv()
+        self.out(self.p, self.total(self.k.x) + self.last[...].astype(F32))
+
+    def drain(self):
+        line = self.line
+        self.over().wait_send()
+        for z, sem in ((line.next, 1), (line.third, 2), (line.two, 3)):
+            self.to(z, 0, sem, 1).wait_send()
 
 
 class LineGradients(Gradients):
@@ -314,14 +418,12 @@
 
     def drain(self, pieces):
         line = self.line
-
-        def piece(p, carry):
+        for p in range(pieces):
+            if p in CROSSED_BACK:
+                continue
             self.one(p).wait_send()
             for z, sem in ((line.next, 1), (line.third, 2), (line.two, 3)):
                 self.to(z, self.far.at[0], sem, 1, p).wait_send()
-            return carry
-
-        lax.fori_loop(0, pieces, piece, 0)
 
 
 class Spread:
@@ -729,6 +831,9 @@
     v_recv,
     load_sem,
     HOP,
+    CFAR,
+    CHOP,
+    CLAST,
     dw_sems,
     dg_sems,
     rc_sems,
@@ -784,6 +889,12 @@
         line = Line(k)
         weights = LineWeights(line, W, w_send, w_recv, width, simple)
         grads = LineGradients(line, HOP, G, near, far, keep, g_send, g_recv, width)
+        crossed = {
+            p: CrossedGradient(
+                line, G, CFAR, CHOP, CLAST, keep, g_send, g_recv, width, p, place
+            )
+            for place, p in enumerate(CROSSED_BACK)
+        }
         down_w = DownWeights(line, W, down_piece * width, inner, dw_sems)
         down_g = DownGradient(line, G, near, far, HOP, down_piece * width, inner, dg_sems)
         w_chunks, g_chunks = down_w.sources, down_g.targets
@@ -828,12 +939,16 @@
     VA[0] = jnp.zeros_like(VA[0])
     if stepped:
         far[2] = jnp.zeros_like(far[2])
+        for place in range(len(CROSSED_BACK)):
+            CFAR[place, 2] = jnp.zeros_like(CFAR[place, 2])
     for copy in loads:
         copy.wait()
     own[:, columns(3, width)] = OT[...].T
     own[:, pl.ds(4 * width + inner, inner)] = DT[...].T
     s0 = spread(X, 0)
     k.enter()
+    if stepped:
+        weights.cross()
     s0.start()
     for p in range(WINDOW):
         weights.start(p)
@@ -853,7 +968,7 @@
         inside = (lane >= h * HEAD_DIM) & (lane < (h + 1) * HEAD_DIM)
         return jnp.where(inside, 1.0, 0.0).astype(BF16)
 
-    def attend(seq):
+    def attend(seq, between=lambda: None):
         ACC[0] = jnp.zeros_like(ACC[0])
 
         def head(h, carry):
@@ -865,7 +980,9 @@
             ACC[0] += dot(probs, V[seq] * mask, TN)
             return carry
 
-        lax.fori_loop(0, heads, head, 0)
+        lax.fori_loop(0, heads // 2, head, 0)
+        between()
+        lax.fori_loop(heads // 2, heads, head, 0)
         C[seq] = ACC[0].astype(BF16)
 
     def out_block(seq, core):
@@ -874,35 +991,34 @@
     relay(0)
     weights.forward(0)
     relay(1)
+    weights.forward(1)
     relay(2)
-    weights.forward(1)
     s0.pass_on()
     s0.own()
     s0.other()
     project(0, Q)
-    relay(3)
     weights.forward(2)
     project(1, K)
-    relay(4)
-    weights.forward(3)
+    relay(3)
+    if not stepped:
+        weights.forward(3)
     project(2, V)
     r0 = reduce(0)
-    attend(theirs)
-    relay(5)
+    attend(theirs, lambda: relay(4))
     weights.forward(4)
     weights.arrive(3)
     r0.across(out_block(theirs, 1 - k.c))
     r0.theirs(out_block(theirs, k.c))
+    relay(5)
+    attend(mine, lambda: weights.forward(5))
     relay(6)
-    attend(mine)
-    weights.forward(5)
-    relay(7)
-    if stepped:
-        down_w.start(1)
     r0.partner(out_block(mine, 1 - k.c))
     r0.mine(out_block(mine, k.c))
     weights.forward(6)
+    relay(7)
     if stepped:
+        down_w.forward(0)
+        down_w.start(1)
         down_w.start(2)
         down_w.start(3)
     r0.wait()
@@ -922,9 +1038,7 @@
     s1 = spread(H, 1)
     s1.start()
     weights.forward(7)
-    if stepped:
-        down_w.forward(0)
-    else:
+    if not stepped:
         weights.forward(8)
     s1.own()
     for p in range(up_piece, down_piece):
@@ -951,8 +1065,8 @@
     if stepped:
         up(mine)
         down_w.forward(1)
+        s1.pass_on()
         down_w.forward(2)
-        s1.pass_on()
         s1.other()
         up(theirs)
         r1 = ReduceColumns(k, OUTBOX, INBOX, OWN, r_send, r_recv, 1, outer, rc_sems)
@@ -1088,8 +1202,10 @@
         down_g.forward(0)
         r2.theirs(hidden_block(theirs, k.c))
         down_g.forward(1)
-        weight_grad(H, GU, up_piece, 0, steps)
-        grads.start(up_piece + steps - 1)
+        weight_grad(H, GU, up_piece, steps - 1, steps)
+        crossed[7].start()
+        weight_grad(H, GU, up_piece, 0, steps - 1)
+        grads.start(up_piece + steps - 2)
         down_g.forward(2)
         down_g.forward(3)
     else:
@@ -1124,7 +1240,7 @@
     s3.start()
     s3.own()
 
-    def attend_back(seq):
+    def attend_back(seq, between=lambda: None):
         GC[...] = dot(pair(GF, seq), matrix(3 * width, width), NN).astype(BF16)
         ACC[...] = jnp.zeros_like(ACC)
 
@@ -1141,7 +1257,9 @@
             ACC[0] += dot(grad, K[seq] * mask, TN)
             return carry
 
-        lax.fori_loop(0, heads, head, 0)
+        lax.fori_loop(0, heads // 2, head, 0)
+        between()
+        lax.fori_loop(heads // 2, heads, head, 0)
         for n in range(3):
             grad = ACC[n] if n == 2 else ACC[n] * scale
             DQKV[seq, :, n * width : (n + 1) * width] = grad.astype(BF16)
@@ -1150,22 +1268,30 @@
         return dot(DQKV[seq, part_rows(core), :], matrix(0, 3 * width), NT)
 
     if stepped:
+        crossed[7].relay()
         grads.forward(4)
-    attend_back(mine)
-    relay_back(4)
-    grads.forward(5 if stepped else 11)
-    s3.pass_on()
-    relay_back(5)
-    grads.forward(6 if stepped else 4)
-    s3.other()
-    weight_grad(GF, C, 3, 0, 1)
-    if not stepped:
+        attend_back(mine)
         grads.forward(5)
-    attend_back(theirs)
-    grads.start(3)
-    relay_back(6)
-    if stepped:
-        grads.forward(7)
+        relay_back(4)
+        s3.pass_on()
+        crossed[7].forward()
+        s3.other()
+        weight_grad(GF, C, 3, 0, 1)
+        grads.forward(6)
+        grads.start(3)
+        relay_back(5)
+        attend_back(theirs)
+        relay_back(6)
+    else:
+        attend_back(mine)
+        grads.forward(11)
+        s3.pass_on()
+        grads.forward(4)
+        s3.other()
+        weight_grad(GF, C, 3, 0, 1)
+        grads.forward(5)
+        attend_back(theirs)
+        grads.start(3)
 
     here = pl.ds(pl.multiple_of(k.t * width, width), width)
     for row, n in ((0, 0), (1, 2)):
@@ -1187,73 +1313,105 @@
         hops[n].wait_recv()
         VA[n + 1] = VA[n] + VR[n]
 
-    weight_grad(X, DQKV, 0, 0, 1)
-    hops[0].start()
-    weight_grad(X, DQKV, 0, 1, 2)
-    grads.start(0)
-    hop_in(0)
-    hops[1].start()
-    weight_grad(X, DQKV, 0, 2, 3)
-    grads.start(1)
-    if not stepped:
+    if stepped:
+        weight_grad(X, DQKV, 0, 2, 3)
+        hops[0].start()
+        crossed[2].start()
+        weight_grad(X, DQKV, 0, 0, 1)
+        hop_in(0)
+        hops[1].start()
+        grads.start(0)
+        weight_grad(X, DQKV, 0, 1, 2)
+        grads.forward(3)
+        grads.start(1)
+    else:
+        weight_grad(X, DQKV, 0, 0, 1)
+        hops[0].start()
+        weight_grad(X, DQKV, 0, 1, 2)
+        grads.start(0)
+        hop_in(0)
+        hops[1].start()
+        weight_grad(X, DQKV, 0, 2, 3)
+        grads.start(1)
         grads.forward(6)
     r3 = reduce(3)
     r3.across(input_block(theirs, 1 - k.c))
+    if stepped:
+        crossed[2].relay()
     r3.theirs(input_block(theirs, k.c))
     hop_in(1)
     hops[2].start()
-    grads.start(2)
-    if not stepped:
+    if stepped:
+        grads.forward(0)
+        relay_back(3)
+    else:
+        grads.start(2)
         grads.forward(7)
     r3.partner(input_block(mine, 1 - k.c))
     r3.mine(input_block(mine, k.c))
-    if not stepped:
-        for p in (8, 9, 10):
-            grads.finish(p)
-    relay_back(7)
-    grads.forward(3)
-    relay_back(3)
-    grads.forward(0)
-    relay_back(0)
-    grads.forward(1)
-    relay_back(1)
-    hop_in(2)
-    VZ[k.z] = VA[3]
 
     def send_last(step, carry):
         vector_last(step).start()
         return carry
 
-    lax.fori_loop(1, outer, send_last, 0)
-    grads.forward(2)
-    relay_back(2)
+    def vectors_along():
+        hop_in(2)
+        VZ[k.z] = VA[3]
+        lax.fori_loop(1, outer, send_last, 0)
+
+    if stepped:
+        crossed[2].forward()
+        relay_back(0)
+        grads.forward(1)
+        vectors_along()
+        relay_back(1)
+    else:
+        for p in (8, 9, 10):
+            grads.finish(p)
+        grads.forward(3)
+        grads.forward(0)
+        grads.forward(1)
+        vectors_along()
+        grads.forward(2)
     r3.wait()
 
     def last(r):
         gin_ref[r, :] = GS[r, :] + r3.total(r)
 
     norm_loop(last)
+    vz_all = VZ.at[pl.ds(0, outer - 1)]
+    every = remote(vz_all, vz_all, v_send.at[3], v_recv.at[3], k.x_peer)
+
+    def add(i, total):
+        return total + VZ[i]
+
+    def vectors_out():
+        every.wait_recv()
+        gvec_ref[...] = lax.fori_loop(1, outer, add, VZ[0])
+
     if stepped:
         down_g.finish(gd_ref)
+        for p in (4, 5, 6):
+            grads.finish(p)
+        crossed[7].finish()
+        for p in (3, 0):
+            grads.finish(p)
+        crossed[2].finish()
+        vectors_out()
+        grads.finish(1)
     else:
-        grads.finish(11)
-    for p in (4, 5, 6, 7, 3, 0, 1):
-        grads.finish(p)
-    vz_all = VZ.at[pl.ds(0, outer - 1)]
-    every = remote(vz_all, vz_all, v_send.at[3], v_recv.at[3], k.x_peer)
-    every.wait_recv()
-
-    def add(i, total):
-        return total + VZ[i]
-
-    gvec_ref[...] = lax.fori_loop(1, outer, add, VZ[0])
-    grads.finish(2)
+        for p in (11, 4, 5, 6, 7, 3, 0, 1):
+            grads.finish(p)
+        vectors_out()
+        grads.finish(2)
 
     weights.drain(simple)
     grads.drain(simple)
     if stepped:
         down_w.drain()
         down_g.drain()
+        for gradient in crossed.values():
+            gradient.drain()
         s2.drain_columns(g_chunks)
     for s in (s0, s1, s3) if stepped else (s0, s1, s2, s3):
         s.drain()
@@ -1339,6 +1497,9 @@
             dma((4,)),
             dma((len(arrays),)),
             pltpu.VMEM((shard_rows, columns_all), BF16),
+            pltpu.VMEM((len(CROSSED_BACK), 3, 2, shard_rows, width), BF16),
+            pltpu.VMEM((len(CROSSED_BACK), 2, shard_rows, width), BF16),
+            pltpu.VMEM((len(CROSSED_BACK), shard_rows, width), BF16),
             (dma((outer, 2)),) * 4,
             (dma((outer,)),) * 4,
             (dma((3, outer)),) * 2,

time: 198 us -> 189 us (0.955)
  Pallas kernels: 194 us -> 186 us
    pallas_call x1, Pallas kernels: 190 us -> 182 us  [layer(): pl.pallas_call(functools.partial(body, outer), out_shape=outs, in_specs=[...]
where the time goes in v5:
time: 189 us
  Pallas kernels  186 us (98%)
  between operations  2.46 us (1%)
    pallas_call x1, Pallas kernels, layer(): pl.pallas_call(functools.partial(body, outer), out_shape=outs, in_specs=[...  182 us

profile of v5, /device:TPU:0, one launch (start us, length us, event | category | flops | bytes accessed | tf_op | source)
XLA Modules:
  0.0 189.3 jit_solution(13050505524223953833)
XLA Ops:
  0.7 181.8 %layer.1 = (bf16[256,1024]{1,0:T(8,128)(2,1)}, f32[256,1024]{1,0:T(8,128)}, f32[128,256]{1,0:T(8,128)}, f32[128,256]{1,0:T(8,128)}, f32[128,256]{1,0:T(8,128)}, ...) custom-call(bf16[256,1024]{1,0:T(8,128)(2,1)} %x_in.1, ...), custom_call_target="tpu_custom_call" | custom-call | tf_op jit(solution)/shard_map/layer/pallas_call | solution.py:1448
  182.5 3.7 %write.1 = (bf16[256,1024]{1,0:T(8,128)(2,1)}, f32[256,1024]{1,0:T(8,128)}, f32[128,256]{1,0:T(8,128)}, f32[128,256]{1,0:T(8,128)}, f32[128,256]{1,0:T(8,128)}, ...) custom-call(bf16[256,1024]{1,0:T(8,128)(2,1)} %get-tuple-element.45., ...), custom_call_target="tpu_custom_call" | custom-call | tf_op jit(solution)/shard_map/write/pallas_call | solution.py:1538
  186.2 0.0 copy-start
  186.2 0.7 copy-done
  186.9 0.6 reduce_sum.9
Async XLA Ops:
  186.2 0.7 copy-start

commit v6 on v5

--- a/solution.py
+++ b/solution.py
@@ -17,8 +17,8 @@
 NN = ((1,), (0,))
 NT = ((1,), (1,))
 TN = ((0,), (0,))
-CHUNK = 32
-WINDOW = 3
+CHUNK = 128
+WINDOW = 2
 CROSSED = (3, 7)
 CROSSED_BACK = (2, 7)
 ROOT_TWO = math.sqrt(2.0)
@@ -219,10 +219,16 @@
         for p in CROSSED:
             self.crossing(p).start()
 
+    def over(self, z, p):
+        block = self.full.at[z, self.k.x, :, columns(p, self.width)]
+        return remote(block, block, self.send.at[1, p], self.recv.at[1, p], self.k.x_peer)
+
     def start(self, p):
         line = self.line
         if p in CROSSED:
             self.crossing(p).wait_recv()
+        else:
+            self.over(self.k.z, p).start()
         self.send_to(line.two, self.k.z, 0, 0, p).start()
         self.send_to(line.next, self.k.z, 0, 0, p).start()
 
@@ -238,13 +244,16 @@
         def _():
             self.send_to(line.next, line.two, 3, 2, p).start()
 
+        if p not in CROSSED:
+            self.over(line.two, p).start()
+            self.over(line.next, p).start()
         if p + WINDOW < self.pieces:
             self.start(p + WINDOW)
 
     def forward(self, p):
         if p not in CROSSED:
             self.some(1, 2, 2, p).wait_recv()
-            self.second(p).start()
+            self.over(self.line.third, p).start()
 
     def arrive(self, p):
         if p in CROSSED:
@@ -350,9 +359,24 @@
 
 
 class LineGradients(Gradients):
-    def __init__(self, line, hop, *rest):
+    def __init__(self, line, hop, x_send, x_recv, *rest):
         super().__init__(line.k, *rest)
-        self.line, self.hop = line, hop
+        self.line, self.hop, self.x_send, self.x_recv = line, hop, x_send, x_recv
+        self.targets = (line.third, line.two, line.next, line.k.z)
+
+    def over(self, p, n):
+        k, z, cols = self.k, self.targets[n], columns(p, self.width)
+        return remote(
+            self.part.at[z, 1 - k.x, :, cols],
+            self.near.at[z, :, cols],
+            self.x_send.at[n, p],
+            self.x_recv.at[n, p],
+            k.x_peer,
+        )
+
+    def start(self, p):
+        for n in range(4):
+            self.over(p, n).start()
 
     def to(self, z, dst, send, recv, p):
         cols = columns(p, self.width)
@@ -376,20 +400,29 @@
 
     def forward(self, p):
         k, line, cols = self.k, self.line, columns(p, self.width)
-        self.one(p).wait_recv()
-        here = self.part[:, k.x, :, cols].astype(F32)
-        self.part[:, k.x, :, cols] = (here + self.near[:, :, cols].astype(F32)).astype(BF16)
-
-        @pl.when(line.end)
-        def _():
-            self.to_hop(p).start()
-            self.to(line.two, self.far.at[0], 3, 1, p).start()
-
-        @pl.when(line.middle)
-        def _():
-            self.to(line.third, self.far.at[2], 2, 2, p).start()
-
-        self.to(line.next, self.far.at[1], 1, 1, p).start()
+        for n in range(4):
+            z = self.targets[n]
+            self.over(p, n).wait_recv()
+            here = self.part[z, k.x, :, cols].astype(F32)
+            self.part[z, k.x, :, cols] = (here + self.near[z, :, cols].astype(F32)).astype(BF16)
+            if n == 0:
+
+                @pl.when(line.end)
+                def _():
+                    self.to_hop(p).start()
+
+                @pl.when(line.middle)
+                def _():
+                    self.to(line.third, self.far.at[2], 2, 2, p).start()
+
+            elif n == 1:
+
+                @pl.when(line.end)
+                def _():
+                    self.to(line.two, self.far.at[0], 3, 1, p).start()
+
+            elif n == 2:
+                self.to(line.next, self.far.at[1], 1, 1, p).start()
 
     def relay(self, p):
         line, cols = self.line, columns(p, self.width)
@@ -421,7 +454,8 @@
         for p in range(pieces):
             if p in CROSSED_BACK:
                 continue
-            self.one(p).wait_send()
+            for n in range(4):
+                self.over(p, n).wait_send()
             for z, sem in ((line.next, 1), (line.third, 2), (line.two, 3)):
                 self.to(z, self.far.at[0], sem, 1, p).wait_send()
 
@@ -600,6 +634,85 @@
         for n, chunk in enumerate(order):
             for number in range(3):
                 self.part(number, n, chunk).wait_send()
+
+
+EARLY_ROWS = {2: (0, 0), 7: (0, 1), 8: (0, 2), 9: (0, 3), 10: (2, 0), 11: (2, 1), 12: (2, 2)}
+EARLY_ROWS.update({3 + n: (1, n) for n in range(4)})
+
+
+class Early:
+    def __init__(self, k, sums, inbox, cross, along, total, sems):
+        self.k, self.sums, self.inbox, self.cross = k, sums, inbox, cross
+        self.along, self.total, (self.send, self.recv) = along, total, sems
+
+    def copy(self, n, src, dst, peer):
+        return remote(src, dst, self.send.at[n], self.recv.at[n], peer)
+
+    def hop(self, n):
+        peer = self.k.c_peer if n == 0 else self.k.y_peer
+        rows = pl.ds(0, 4)
+        return self.copy(n, self.sums.at[n, :, rows], self.inbox.at[n, :, rows], peer)
+
+    def over(self):
+        rows = pl.ds(0, 4)
+        return self.copy(
+            2, self.sums.at[2, self.k.t, rows], self.cross.at[0, rows], self.k.x_peer
+        )
+
+    def last(self, step):
+        rows = pl.ds(0, 4)
+        return self.copy(
+            3, self.cross.at[1, rows], self.along.at[self.k.z, rows], self.k.z_peer(step)
+        )
+
+    def every(self):
+        block = self.along.at[pl.ds(0, self.k.outer - 1), pl.ds(0, 4)]
+        return self.copy(3, block, block, self.k.x_peer)
+
+    def share(self, n):
+        k = self.k
+        block = self.total.at[k.t, pl.ds(0, 4)]
+        return self.copy(4 + n, block, block, (k.c_peer, k.y_peer, k.diag_peer)[n])
+
+    def add(self, n):
+        self.hop(n).wait_recv()
+        self.sums[n + 1, :, 0:4, :] = self.sums[n, :, 0:4, :] + self.inbox[n, :, 0:4, :]
+
+    def add_over(self):
+        k = self.k
+        self.over().wait_recv()
+        total = self.sums[2, k.t, 0:4, :] + self.cross[0, 0:4, :]
+        self.cross[1, 0:4, :] = total
+        self.along[k.z, 0:4, :] = total
+
+        def send(step, carry):
+            self.last(step).start()
+            return carry
+
+        lax.fori_loop(1, k.outer, send, 0)
+
+    def add_along(self):
+        self.every().wait_recv()
+
+        def add(i, total):
+            return total + self.along[i, 0:4, :]
+
+        first = self.along[0, 0:4, :]
+        self.total[self.k.t, 0:4, :] = lax.fori_loop(1, self.k.outer, add, first)
+        for n in range(3):
+            self.share(n).start()
+
+    def finish(self):
+        for n in range(3):
+            self.share(n).wait_recv()
+
+    def drain(self):
+        self.hop(0).wait_send()
+        self.hop(1).wait_send()
+        self.over().wait_send()
+        self.every().wait_send()
+        for n in range(3):
+            self.share(n).wait_send()
 
 
 class DownWeights:
@@ -815,6 +928,11 @@
     VA,
     VR,
     VZ,
+    EA,
+    EC,
+    EX,
+    EZ,
+    ET,
     TEACH,
     OT,
     DT,
@@ -834,6 +952,9 @@
     CFAR,
     CHOP,
     CLAST,
+    gx_send,
+    gx_recv,
+    early_sems,
     dw_sems,
     dg_sems,
     rc_sems,
@@ -888,7 +1009,7 @@
     if stepped:
         line = Line(k)
         weights = LineWeights(line, W, w_send, w_recv, width, simple)
-        grads = LineGradients(line, HOP, G, near, far, keep, g_send, g_recv, width)
+        grads = LineGradients(line, HOP, gx_send, gx_recv, G, near, far, keep, g_send, g_recv, width)
         crossed = {
             p: CrossedGradient(
                 line, G, CFAR, CHOP, CLAST, keep, g_send, g_recv, width, p, place
@@ -937,21 +1058,24 @@
 
     SUMS[...] = jnp.zeros_like(SUMS)
     VA[0] = jnp.zeros_like(VA[0])
+    EA[0] = jnp.zeros_like(EA[0])
     if stepped:
         far[2] = jnp.zeros_like(far[2])
         for place in range(len(CROSSED_BACK)):
             CFAR[place, 2] = jnp.zeros_like(CFAR[place, 2])
-    for copy in loads:
+    for copy in loads[:4]:
+        copy.wait()
+    s0 = spread(X, 0)
+    k.enter()
+    for p in range(WINDOW):
+        weights.start(p)
+    s0.start()
+    for copy in loads[4:]:
         copy.wait()
     own[:, columns(3, width)] = OT[...].T
     own[:, pl.ds(4 * width + inner, inner)] = DT[...].T
-    s0 = spread(X, 0)
-    k.enter()
     if stepped:
         weights.cross()
-    s0.start()
-    for p in range(WINDOW):
-        weights.start(p)
 
     def project(p, held):
         weights.arrive(p)
@@ -1197,9 +1321,9 @@
             s2.other_part(n, g_chunks[n])
             down_grad_chunk(n)
             down_g.start(n)
+        down_g.forward(0)
         back_up(theirs)
         r2.across(hidden_block(theirs, 1 - k.c))
-        down_g.forward(0)
         r2.theirs(hidden_block(theirs, k.c))
         down_g.forward(1)
         weight_grad(H, GU, up_piece, steps - 1, steps)
@@ -1238,6 +1362,12 @@
     norm_loop(first_back)
     s3 = spread(GF, 3)
     s3.start()
+    early = Early(k, EA, EC, EX, EZ, ET, early_sems)
+    for n, row in ((4, 2), (0, 7), (5, 8), (6, 9), (1, 10), (2, 11), (3, 12)):
+        group, place = EARLY_ROWS[row]
+        EA[0, group, place : place + 1, :] = jnp.sum(SUMS[n], axis=0, keepdims=True)
+    EA[0, 1, pl.ds(k.t, 1), :] = jnp.sum(SUMS[7], axis=0, keepdims=True)
+    early.hop(0).start()
     s3.own()
 
     def attend_back(seq, between=lambda: None):
@@ -1271,6 +1401,8 @@
         crossed[7].relay()
         grads.forward(4)
         attend_back(mine)
+        early.add(0)
+        early.hop(1).start()
         grads.forward(5)
         relay_back(4)
         s3.pass_on()
@@ -1278,18 +1410,24 @@
         s3.other()
         weight_grad(GF, C, 3, 0, 1)
         grads.forward(6)
+        early.add(1)
+        early.over().start()
         grads.start(3)
         relay_back(5)
         attend_back(theirs)
         relay_back(6)
     else:
         attend_back(mine)
+        early.add(0)
+        early.hop(1).start()
         grads.forward(11)
         s3.pass_on()
         grads.forward(4)
         s3.other()
         weight_grad(GF, C, 3, 0, 1)
         grads.forward(5)
+        early.add(1)
+        early.over().start()
         attend_back(theirs)
         grads.start(3)
 
@@ -1297,21 +1435,24 @@
     for row, n in ((0, 0), (1, 2)):
         grad = DQKV[:, :, n * width : (n + 1) * width].reshape(4 * rows, width).astype(F32)
         VA[0, row : row + 1, here] = jnp.sum(grad, axis=0, keepdims=True)
-    VA[0, pl.ds(3 + k.t, 1), :] = jnp.sum(SUMS[7], axis=0, keepdims=True)
-    for row, n in ((7, 0), (10, 1), (11, 2), (12, 3), (2, 4), (8, 5), (9, 6)):
-        VA[0, row : row + 1, :] = jnp.sum(SUMS[n], axis=0, keepdims=True)
+
+    two_rows = pl.ds(0, 2)
 
     def vector_hop(n, peer):
-        return remote(VA.at[n], VR.at[n], v_send.at[n], v_recv.at[n], peer)
+        return remote(
+            VA.at[n, two_rows], VR.at[n, two_rows], v_send.at[n], v_recv.at[n], peer
+        )
 
     def vector_last(step):
-        return remote(VA.at[3], VZ.at[k.z], v_send.at[3], v_recv.at[3], k.z_peer(step))
+        return remote(
+            VA.at[3, two_rows], VZ.at[k.z, two_rows], v_send.at[3], v_recv.at[3], k.z_peer(step)
+        )
 
     hops = [vector_hop(n, peer) for n, peer in enumerate((k.c_peer, k.y_peer, k.x_peer))]
 
     def hop_in(n):
         hops[n].wait_recv()
-        VA[n + 1] = VA[n] + VR[n]
+        VA[n + 1, 0:2, :] = VA[n, 0:2, :] + VR[n, 0:2, :]
 
     if stepped:
         weight_grad(X, DQKV, 0, 2, 3)
@@ -1322,8 +1463,8 @@
         hops[1].start()
         grads.start(0)
         weight_grad(X, DQKV, 0, 1, 2)
+        early.add_over()
         grads.forward(3)
-        grads.start(1)
     else:
         weight_grad(X, DQKV, 0, 0, 1)
         hops[0].start()
@@ -1337,14 +1478,16 @@
     r3 = reduce(3)
     r3.across(input_block(theirs, 1 - k.c))
     if stepped:
+        grads.start(1)
         crossed[2].relay()
     r3.theirs(input_block(theirs, k.c))
     hop_in(1)
     hops[2].start()
     if stepped:
+        relay_back(3)
         grads.forward(0)
-        relay_back(3)
     else:
+        early.add_over()
         grads.start(2)
         grads.forward(7)
     r3.partner(input_block(mine, 1 - k.c))
@@ -1356,14 +1499,15 @@
 
     def vectors_along():
         hop_in(2)
-        VZ[k.z] = VA[3]
+        VZ[k.z, 0:2, :] = VA[3, 0:2, :]
         lax.fori_loop(1, outer, send_last, 0)
 
+    early.add_along()
     if stepped:
-        crossed[2].forward()
         relay_back(0)
         grads.forward(1)
         vectors_along()
+        crossed[2].forward()
         relay_back(1)
     else:
         for p in (8, 9, 10):
@@ -1379,15 +1523,18 @@
         gin_ref[r, :] = GS[r, :] + r3.total(r)
 
     norm_loop(last)
-    vz_all = VZ.at[pl.ds(0, outer - 1)]
+    vz_all = VZ.at[pl.ds(0, outer - 1), two_rows]
     every = remote(vz_all, vz_all, v_send.at[3], v_recv.at[3], k.x_peer)
 
     def add(i, total):
-        return total + VZ[i]
+        return total + VZ[i, 0:2, :]
 
     def vectors_out():
         every.wait_recv()
-        gvec_ref[...] = lax.fori_loop(1, outer, add, VZ[0])
+        gvec_ref[0:2, :] = lax.fori_loop(1, outer, add, VZ[0, 0:2, :])
+        early.finish()
+        for row, (group, place) in EARLY_ROWS.items():
+            gvec_ref[row : row + 1, :] = ET[group, place : place + 1, :]
 
     if stepped:
         down_g.finish(gd_ref)
@@ -1419,6 +1566,7 @@
     for hop in hops:
         hop.wait_send()
     every.wait_send()
+    early.drain()
 
 
 def layer(outer, arrays):
@@ -1478,9 +1626,14 @@
             pltpu.VMEM((3, seq, width), F32),
             pltpu.VMEM((3, rows, model), BF16),
             pltpu.VMEM((3, rows, model), BF16),
-            pltpu.VMEM((4, VECTORS, model), F32),
-            pltpu.VMEM((3, VECTORS, model), F32),
-            pltpu.VMEM((outer, VECTORS, model), F32),
+            pltpu.VMEM((4, 8, model), F32),
+            pltpu.VMEM((3, 8, model), F32),
+            pltpu.VMEM((outer, 8, model), F32),
+            pltpu.VMEM((3, 4, 8, model), F32),
+            pltpu.VMEM((2, 4, 8, model), F32),
+            pltpu.VMEM((2, 8, model), F32),
+            pltpu.VMEM((outer, 8, model), F32),
+            pltpu.VMEM((4, 8, model), F32),
             pltpu.VMEM((rows, model), BF16),
             pltpu.VMEM((width, shard_rows), BF16),
             pltpu.VMEM((inner, shard_rows), BF16),
@@ -1500,6 +1653,9 @@
             pltpu.VMEM((len(CROSSED_BACK), 3, 2, shard_rows, width), BF16),
             pltpu.VMEM((len(CROSSED_BACK), 2, shard_rows, width), BF16),
             pltpu.VMEM((len(CROSSED_BACK), shard_rows, width), BF16),
+            dma((4, pieces)),
+            dma((4, pieces)),
+            (dma((7,)),) * 2,
             (dma((outer, 2)),) * 4,
             (dma((outer,)),) * 4,
             (dma((3, outer)),) * 2,
@@ -1512,11 +1668,11 @@
     )(*arrays)
 
 
-def write_body(count, *refs):
+def write_body(count, factor, *refs):
     ins, outs, sem = refs[:9], refs[9 : 9 + count], refs[-1]
     vec = ins[8]
     pairs = list(zip(ins[:8], outs[:8]))
-    single = [(0, 8), (1, 9), (2, 10), (7, 12), (8, 13), (9, 14), (10, 15), (11, 16), (12, 17)]
+    single = [(0, 8), (1, 9), (2, 10), (7, 12), (8, 13), (9, 14), (10, 15), (11, 16)]
     pairs += [(vec.at[pl.ds(row, 1), :], outs[place]) for row, place in single]
     model = vec.shape[1]
     parts = outs[11].shape[1] // model
@@ -1525,21 +1681,24 @@
     copies = [pltpu.make_async_copy(src, dst, sem.at[n]) for n, (src, dst) in enumerate(pairs)]
     for copy in copies:
         copy.start()
+    outs[17][0, 0] = jnp.sum(vec[12:13, :]) * factor
     for copy in copies:
         copy.wait()
 
 
-def write(values, up_length):
+def write(values, up_length, factor):
     model = values[8].shape[1]
     line = jax.ShapeDtypeStruct((1, model), F32)
     outs = [jax.ShapeDtypeStruct(v.shape, v.dtype) for v in values[:8]] + [line] * 10
     outs[11] = jax.ShapeDtypeStruct((1, up_length), F32)
-    copies = 17 + up_length // model
+    outs[17] = jax.ShapeDtypeStruct((1, 1), F32)
+    copies = 16 + up_length // model
     return pl.pallas_call(
-        functools.partial(write_body, len(outs)),
+        functools.partial(write_body, len(outs), factor),
         out_shape=tuple(outs),
         in_specs=[pl.BlockSpec(memory_space=pltpu.VMEM)] * len(values),
-        out_specs=(pl.BlockSpec(memory_space=pl.ANY),) * len(outs),
+        out_specs=(pl.BlockSpec(memory_space=pl.ANY),) * 17
+        + (pl.BlockSpec(memory_space=pltpu.SMEM),),
         scratch_shapes=[pltpu.SemaphoreType.DMA((copies,))],
         name="write",
     )(*values)
@@ -1550,9 +1709,9 @@
     outer = lax.axis_size("dp") // 2
     arrays = arrays[:8] + tuple(v.reshape(1, -1) for v in arrays[8:])
     up_length = arrays[11].shape[1]
-    values = write(layer(outer, arrays), up_length)
     token_total = inputs.shape[0] * lax.axis_size("dp") * lax.axis_size("tensor")
-    loss = jnp.sum(values[17]) * (0.5 / token_total)
+    values = write(layer(outer, arrays), up_length, 0.5 / token_total)
+    loss = values[17].reshape(())
     output, grad_inputs, gq, gk, gv, go, gu, gd = values[:8]
     return (output, loss, grad_inputs, gq, gk, gv, go, gu, gd) + tuple(
         v.reshape(-1) for v in values[8:17]

time: 189 us -> 178 us (0.942)
  Pallas kernels: 186 us -> 177 us
    pallas_call x1, Pallas kernels: 182 us -> 173 us  [layer(): pl.pallas_call(functools.partial(body, outer), out_shape=outs, in_specs=[...]
where the time goes in v6:
time: 178 us
  Pallas kernels  177 us (99%)
    pallas_call x1, Pallas kernels, layer(): pl.pallas_call(functools.partial(body, outer), out_shape=outs, in_specs=[...  173 us
    pallas_call x1, Pallas kernels, write(): pl.pallas_call(functools.partial(write_body, len(outs), factor), out_shap...  4.22 us

profile of v6, /device:TPU:0, one launch (start us, length us, event | category | flops | bytes accessed | tf_op | source)
XLA Modules:
  0.0 177.7 jit_solution(11760408404931899775)
XLA Ops:
  0.7 172.6 %layer.1 = (bf16[256,1024]{1,0:T(8,128)(2,1)}, f32[256,1024]{1,0:T(8,128)}, f32[128,256]{1,0:T(8,128)}, f32[128,256]{1,0:T(8,128)}, f32[128,256]{1,0:T(8,128)}, ...) custom-call(bf16[256,1024]{1,0:T(8,128)(2,1)} %x_in.1, ...), custom_call_target="tpu_custom_call" | custom-call | tf_op jit(solution)/shard_map/layer/pallas_call | solution.py:1596
  173.3 4.2 %write.1 = (bf16[256,1024]{1,0:T(8,128)(2,1)}, f32[256,1024]{1,0:T(8,128)}, f32[128,256]{1,0:T(8,128)}, f32[128,256]{1,0:T(8,128)}, f32[128,256]{1,0:T(8,128)}, ...) custom-call(bf16[256,1024]{1,0:T(8,128)(2,1)} %get-tuple-element.45., ...), custom_call_target="tpu_custom_call" | custom-call | tf_op jit(solution)/shard_map/write/pallas_call | solution.py:1696

commit v7 on v6

--- a/solution.py
+++ b/solution.py
@@ -889,6 +889,15 @@
     b1_in,
     g2_in,
     b2_in,
+    out_hbm,
+    gin_hbm,
+    gq_hbm,
+    gk_hbm,
+    gv_hbm,
+    go_hbm,
+    gu_hbm,
+    gd_hbm,
+    gvec_hbm,
     out_ref,
     gin_ref,
     gq_ref,
@@ -917,10 +926,8 @@
     ACT,
     GU,
     OWN,
-    HID,
     N1,
     R1,
-    GS,
     SUMS,
     ACC,
     OUTBOX,
@@ -948,6 +955,7 @@
     v_send,
     v_recv,
     load_sem,
+    flush_sem,
     HOP,
     CFAR,
     CHOP,
@@ -994,11 +1002,28 @@
     k.greet()
 
 
+    results = (
+        (out_ref, out_hbm),
+        (gin_ref, gin_hbm),
+        (gq_ref, gq_hbm),
+        (gk_ref, gk_hbm),
+        (gv_ref, gv_hbm),
+        (go_ref, go_hbm),
+        (gu_ref, gu_hbm),
+        (gd_ref, gd_hbm),
+        (gvec_ref, gvec_hbm),
+    )
+
+    def flush(n):
+        return pltpu.make_async_copy(*results[n], flush_sem.at[n])
+
     def keep(p, total):
         if p < 3:
             (gq_ref, gk_ref, gv_ref)[p][...] = total
+            flush(2 + p).start()
         elif p == 3:
             go_ref[...] = total.T
+            flush(5).start()
         elif p < down_piece:
             gu_ref[:, (p - up_piece) * width : (p - up_piece + 1) * width] = total
         else:
@@ -1155,7 +1180,7 @@
         hidden = normed * vector(4) + vector(5)
         N1[r, :] = normed
         R1[r, :] = jnp.broadcast_to(scaling, (CHUNK, R1.shape[1]))
-        HID[r, :] = hidden
+        gin_ref[r, :] = hidden
         H[k.t, r, :] = hidden.astype(BF16)
 
     norm_loop(first_norm)
@@ -1240,7 +1265,7 @@
         return scaling * (e - mean(e) - normed * mean(e * normed))
 
     def second_norm(r):
-        second = HID[r, :] + r1.total(r) + vector(3)
+        second = gin_ref[r, :] + r1.total(r) + vector(3)
         center = second - mean(second)
         scaling = lax.rsqrt(mean(center * center) + EPSILON)
         normed = center * scaling
@@ -1248,7 +1273,7 @@
         out_ref[r, :] = result.astype(BF16)
         diff = result - TEACH[r, :].astype(F32)
         grad = norm_back(diff, vector(6), normed, scaling)
-        GS[r, :] = grad
+        gin_ref[r, :] = grad
         MX[k.t, r, :] = grad.astype(BF16)
         SUMS[0] += fold(grad)
         SUMS[1] += fold(diff * normed)
@@ -1256,6 +1281,7 @@
         SUMS[3] += fold(diff * diff)
 
     norm_loop(second_norm)
+    flush(0).start()
     if stepped:
         s2 = SpreadColumns(k, MX, s_send, s_recv, 2, outer, sc_sems)
         s2.start_columns(g_chunks)
@@ -1350,10 +1376,10 @@
     r2.wait()
 
     def first_back(r):
-        grad_hidden = GS[r, :] + r2.total(r)
+        grad_hidden = gin_ref[r, :] + r2.total(r)
         normed = N1[r, :]
         grad = norm_back(grad_hidden, vector(4), normed, R1[r, :][:, :1])
-        GS[r, :] = grad
+        gin_ref[r, :] = grad
         GF[k.t, r, :] = grad.astype(BF16)
         SUMS[4] += fold(grad)
         SUMS[5] += fold(grad_hidden * normed)
@@ -1520,9 +1546,10 @@
     r3.wait()
 
     def last(r):
-        gin_ref[r, :] = GS[r, :] + r3.total(r)
+        gin_ref[r, :] = gin_ref[r, :] + r3.total(r)
 
     norm_loop(last)
+    flush(1).start()
     vz_all = VZ.at[pl.ds(0, outer - 1), two_rows]
     every = remote(vz_all, vz_all, v_send.at[3], v_recv.at[3], k.x_peer)
 
@@ -1535,12 +1562,15 @@
         early.finish()
         for row, (group, place) in EARLY_ROWS.items():
             gvec_ref[row : row + 1, :] = ET[group, place : place + 1, :]
+        flush(8).start()
 
     if stepped:
         down_g.finish(gd_ref)
+        flush(7).start()
         for p in (4, 5, 6):
             grads.finish(p)
         crossed[7].finish()
+        flush(6).start()
         for p in (3, 0):
             grads.finish(p)
         crossed[2].finish()
@@ -1549,6 +1579,8 @@
     else:
         for p in (11, 4, 5, 6, 7, 3, 0, 1):
             grads.finish(p)
+        flush(6).start()
+        flush(7).start()
         vectors_out()
         grads.finish(2)
 
@@ -1567,6 +1599,8 @@
         hop.wait_send()
     every.wait_send()
     early.drain()
+    for n in range(len(results)):
+        flush(n).wait()
 
 
 def layer(outer, arrays):
@@ -1578,7 +1612,6 @@
     columns_all = 4 * width + 2 * inner
     pieces = columns_all // width
     seq = 2 * rows
-    vmem = pl.BlockSpec(memory_space=pltpu.VMEM)
     anywhere = pl.BlockSpec(memory_space=pl.ANY)
     full = (outer, 2, shard_rows, columns_all)
     dma = pltpu.SemaphoreType.DMA
@@ -1597,8 +1630,9 @@
         functools.partial(body, outer),
         out_shape=outs,
         in_specs=[anywhere] * len(arrays),
-        out_specs=(vmem,) * len(outs),
-        scratch_shapes=[
+        out_specs=(anywhere,) * len(outs),
+        scratch_shapes=[pltpu.VMEM(out.shape, out.dtype) for out in outs]
+        + [
             pltpu.VMEM(full, BF16),
             pltpu.VMEM(full, BF16),
             pltpu.VMEM((outer, shard_rows, columns_all), BF16),
@@ -1619,9 +1653,7 @@
             pltpu.VMEM((2, seq, inner), BF16),
             pltpu.VMEM((rows, model), F32),
             pltpu.VMEM((rows, model), F32),
-            pltpu.VMEM((rows, model), F32),
             pltpu.VMEM((rows, 128), F32),
-            pltpu.VMEM((rows, model), F32),
             pltpu.VMEM((8, 8, model), F32),
             pltpu.VMEM((3, seq, width), F32),
             pltpu.VMEM((3, rows, model), BF16),
@@ -1649,6 +1681,7 @@
             dma((4,)),
             dma((4,)),
             dma((len(arrays),)),
+            dma((len(outs),)),
             pltpu.VMEM((shard_rows, columns_all), BF16),
             pltpu.VMEM((len(CROSSED_BACK), 3, 2, shard_rows, width), BF16),
             pltpu.VMEM((len(CROSSED_BACK), 2, shard_rows, width), BF16),
@@ -1669,9 +1702,13 @@
 
 
 def write_body(count, factor, *refs):
-    ins, outs, sem = refs[:9], refs[9 : 9 + count], refs[-1]
-    vec = ins[8]
-    pairs = list(zip(ins[:8], outs[:8]))
+    ins, outs = refs[:9], refs[9 : 9 + count]
+    held, load_sem, sem = refs[9 + count : 18 + count], refs[-2], refs[-1]
+    loads = [
+        pltpu.make_async_copy(src, dst, load_sem.at[n]) for n, (src, dst) in enumerate(zip(ins, held))
+    ]
+    vec = held[8]
+    pairs = list(zip(held[:8], outs[:8]))
     single = [(0, 8), (1, 9), (2, 10), (7, 12), (8, 13), (9, 14), (10, 15), (11, 16)]
     pairs += [(vec.at[pl.ds(row, 1), :], outs[place]) for row, place in single]
     model = vec.shape[1]
@@ -1679,8 +1716,13 @@
     for n in range(parts):
         pairs.append((vec.at[pl.ds(3 + n, 1), :], outs[11].at[:, pl.ds(n * model, model)]))
     copies = [pltpu.make_async_copy(src, dst, sem.at[n]) for n, (src, dst) in enumerate(pairs)]
-    for copy in copies:
-        copy.start()
+    order = (8, 5, 2, 3, 4, 6, 7, 0, 1)
+    for n in order:
+        loads[n].start()
+    for n in order:
+        loads[n].wait()
+        for copy in copies[8:] if n == 8 else copies[n : n + 1]:
+            copy.start()
     outs[17][0, 0] = jnp.sum(vec[12:13, :]) * factor
     for copy in copies:
         copy.wait()
@@ -1693,13 +1735,14 @@
     outs[11] = jax.ShapeDtypeStruct((1, up_length), F32)
     outs[17] = jax.ShapeDtypeStruct((1, 1), F32)
     copies = 16 + up_length // model
+    anywhere = pl.BlockSpec(memory_space=pl.ANY)
     return pl.pallas_call(
         functools.partial(write_body, len(outs), factor),
         out_shape=tuple(outs),
-        in_specs=[pl.BlockSpec(memory_space=pltpu.VMEM)] * len(values),
-        out_specs=(pl.BlockSpec(memory_space=pl.ANY),) * 17
-        + (pl.BlockSpec(memory_space=pltpu.SMEM),),
-        scratch_shapes=[pltpu.SemaphoreType.DMA((copies,))],
+        in_specs=[anywhere] * len(values),
+        out_specs=(anywhere,) * 17 + (pl.BlockSpec(memory_space=pltpu.SMEM),),
+        scratch_shapes=[pltpu.VMEM(v.shape, v.dtype) for v in values]
+        + [pltpu.SemaphoreType.DMA((len(values),)), pltpu.SemaphoreType.DMA((copies,))],
         name="write",
     )(*values)
 

time: 178 us -> 176 us (0.989)
  Pallas kernels: 177 us -> 175 us
where the time goes in v7:
time: 176 us
  Pallas kernels  175 us (99%)
    pallas_call x1, Pallas kernels, layer(): pl.pallas_call(functools.partial(body, outer), out_shape=outs, in_specs=[...  171 us
    pallas_call x1, Pallas kernels, write(): pl.pallas_call(functools.partial(write_body, len(outs), factor), out_shap...  4 us

profile of v7, /device:TPU:0, one launch (start us, length us, event | category | flops | bytes accessed | tf_op | source)
XLA Modules:
  0.0 176.3 jit_solution(13655855535129270688)
XLA Ops:
  0.7 171.5 %layer.1 = (bf16[256,1024]{1,0:T(8,128)(2,1)}, f32[256,1024]{1,0:T(8,128)}, f32[128,256]{1,0:T(8,128)}, f32[128,256]{1,0:T(8,128)}, f32[128,256]{1,0:T(8,128)}, ...) custom-call(bf16[256,1024]{1,0:T(8,128)(2,1)} %x_in.1, ...), custom_call_target="tpu_custom_call" | custom-call | tf_op jit(solution)/shard_map/layer/pallas_call | solution.py:1629
  172.1 4.0 %write.1 = (bf16[256,1024]{1,0:T(8,128)(2,1)}, f32[256,1024]{1,0:T(8,128)}, f32[128,256]{1,0:T(8,128)}, f32[128,256]{1,0:T(8,128)}, f32[128,256]{1,0:T(8,128)}, ...) custom-call(bf16[256,1024]{1,0:T(8,128)(2,1)} %get-tuple-element.45., ...), custom_call_target="tpu_custom_call" | custom-call | tf_op jit(solution)/shard_map/write/pallas_call | solution.py:1739
